TPU v7x, 512 devices: a whole 4x4x16 slice. The times are simulated.
512 devices in a mesh: section: 4 (over y), band: 128 (over z, x, core).
Axes of the slice: x: 4, y: 4, z: 16, core: 2. Of those that a mesh axis runs over, the one named last changes fastest.
Arguments:
- control: bfloat16 [4, 512, 2, 128, 512], P('section', 'band'), may hold values from -6 to 6
- legendre: bfloat16 [512, 512, 512], P('band'), may hold values from -0.25 to 0.25
- spectral_sd: float32 [4, 512], P('section'), may hold values from 0.3 to 3
- vertical: bfloat16 [4, 128, 128], P('section'), may hold values from -0.5 to 0.5
- obs_lon: int32 [512, 1024], P('band'), may hold values from 0 to 1023
- obs_count: int32 [512], P('band'), may hold values from 1 to 1024, as said below
- kernels: bfloat16 [512, 1024, 128], P('band'), may hold values from 0 to 0.0039978027
- obs_value: float32 [512, 1024], P('band'), may hold values from -8 to 8
- obs_weight: float32 [512, 1024], P('band'), may hold values from 1 to 16
Outputs:
- gradient: bfloat16 [4, 512, 2, 128, 512], P('section', 'band')
- departures: float32 [512, 1024], P('band')
Inputs may be any that keep to these rules, and one draw needn't show every extreme that they name: Slots 0 to obs_count - 1 of a latitude row hold its soundings, the others are empty; some row holds exactly 1024.
All inputs are finite; a program needn't handle non-finite values.
Results may differ from a plain program's by a relative error of at most 0.014.
Values may be sent and summed in bfloat16 or wider, within the bound.
No kernel may reach another device: no remote copies, remote signals or barrier semaphores. Data moves between devices by JAX's collectives and lax.ppermute only.
A program may use at most 64 MiB of HBM per device.

v0:
```python
import math

import jax
import jax.numpy as jnp
from jax import lax
from jax.sharding import PartitionSpec as P

M = 512
NLON = 1024


def make_basis(longitude):
    wave_ids = jnp.arange(M, dtype=jnp.int32)
    phase_idx = longitude[..., None] * wave_ids % NLON
    angles = phase_idx.astype(jnp.float32) * (2.0 * math.pi / NLON)
    wave_weight = jnp.where(wave_ids == 0, 1.0, 2.0).astype(jnp.float32)
    fourier = jnp.stack([wave_weight * jnp.cos(angles), -wave_weight * jnp.sin(angles)], axis=-2)
    return fourier.astype(jnp.bfloat16)


def observe(evolved, fourier, counts, kern_rows, value_rows, weight_rows):
    slot_ids = lax.broadcasted_iota(jnp.int32, evolved.shape, 1)
    is_live = slot_ids < counts[:, None]
    departures = jnp.where(is_live, evolved - value_rows, jnp.float32(0.0))
    adjoint_columns = (
        (weight_rows * departures)[:, :, None] * kern_rows.astype(jnp.float32)
    ).astype(jnp.bfloat16)
    adjoint_fields = jnp.einsum(
        "jqrm,jql->mjrl", fourier, adjoint_columns, preferred_element_type=jnp.float32
    )
    return (departures, adjoint_fields.astype(jnp.bfloat16))


def local(
    control, legendre, spectral_sd, vertical, obs_lon, obs_count, kernels, obs_value, obs_weight
):
    coeffs = control[0]
    spread = spectral_sd[0]
    mixing = vertical[0]
    scaled = (coeffs.astype(jnp.float32) * spread).astype(jnp.bfloat16)
    spectral_rows = jnp.einsum(
        "mnj,mrkn->mjrk", legendre, scaled, preferred_element_type=jnp.float32
    ).astype(jnp.bfloat16)
    fields = jnp.einsum(
        "mjrk,lk->mjrl", spectral_rows, mixing, preferred_element_type=jnp.float32
    ).astype(jnp.bfloat16)
    fourier = make_basis(obs_lon)
    columns = jnp.einsum(
        "jqrm,mjrl->jql",
        fourier,
        lax.all_to_all(fields, "band", split_axis=1, concat_axis=0, tiled=True),
        preferred_element_type=jnp.float32,
    )
    partial_obs = jnp.sum(kernels.astype(jnp.float32) * columns, axis=2)
    evolved = lax.psum(partial_obs, "section")
    departures, adjoint_fields = observe(
        evolved, fourier, obs_count, kernels, obs_value, obs_weight
    )
    back_rows = jnp.einsum(
        "mjrl,lk->mjrk",
        lax.all_to_all(adjoint_fields, "band", split_axis=0, concat_axis=1, tiled=True),
        mixing,
        preferred_element_type=jnp.float32,
    ).astype(jnp.bfloat16)
    gradient_terms = jnp.einsum(
        "mjrk,mnj->mrkn", back_rows, legendre, preferred_element_type=jnp.float32
    )
    gradient = (coeffs.astype(jnp.float32) + spread * gradient_terms).astype(jnp.bfloat16)
    return (gradient[None], departures)


def solution(mesh):
    in_specs = (
        P("section", "band", None, None, None),
        P("band", None, None),
        P("section", None),
        P("section", None, None),
        P("band", None),
        P("band"),
        P("band", None, None),
        P("band", None),
        P("band", None),
    )
    out_specs = (P("section", "band", None, None, None), P("band", None))
    return jax.shard_map(local, mesh=mesh, in_specs=in_specs, out_specs=out_specs, check_vma=False)
```

profile of v0, /device:TPU:32, one launch (start us, length us, event | category | flops | bytes accessed | tf_op | source)
XLA Modules:
  0.0 180.4 jit_solution(10526467798709174556)
XLA Ops:
  0.6 0.0 copy-start
  0.6 1.6 copy-done
  2.2 2.2 %convolution_convert_fusion.1 = bf16[4,512,2,128]{3,1,2,0:T(8,128)(2,1)S(1)} fusion(bf16[4,512,512]{2,1,0:T(8,128)(2,1)S(1)} %copy-done, bf16[1,4,2,128,512]{4,3,2,1,0:T(8,128)(2,1)} %param.9, f32[512]{0:T(512)} %bitcast.66, bf16[1,128,128]{2,1,0:T(8,128)(2,1)} %param.12), kind=kOutput, calls=%fused_computation.29 | convolution fusion | flops 673710080 | bytes 4229120 | tf_op jit(solution)/shard_map/mjrk,lk->mjrl/dot_general | solution.py:44
  4.5 0.0 copy-start.3
  4.5 2.1 %copy.20 = bf16[4,512,2,128]{3,2,0,1:T(2,128)(2,1)} copy(bf16[4,512,2,128]{3,1,2,0:T(8,128)(2,1)S(1)} %convolution_convert_fusion.1) | data formatting | bytes 2097152 | tf_op jit(solution)/shard_map/convert_element_type | solution.py:46
  6.6 19.0 %all-to-all-start = ((bf16[4,512,2,128]{3,2,0,1:T(2,128)(2,1)}), bf16[4,512,2,128]{3,2,0,1:T(2,128)(2,1)S(1)}, u32[]{:S(2)}, u32[]{:S(2)}) async-start(bf16[4,512,2,128]{3,2,0,1:T(2,128)(2,1)} %copy.20), calls=%async_computation | async-start | bytes 2097152 | tf_op jit(solution)/shard_map/all_to_all | solution.py:51
  25.6 2.3 %copy.18 = bf16[4,1024,128]{1,2,0:T(8,128)(2,1)} copy(bf16[4,1024,128]{2,1,0:T(8,128)(2,1)} %param.15) | data formatting | bytes 2097152 | tf_op args[6]
  27.9 0.0 copy-done.3
  27.9 36.7 %multiply_convert_fusion.1 = (bf16[4,1024,1,512]{3,1,2,0:T(8,128)(2,1)}, bf16[4,1024,1,512]{3,1,2,0:T(8,128)(2,1)}) fusion(s32[4,1024]{1,0:T(4,128)S(1)} %copy-done.3, f32[512]{0:T(512)S(1)} %get-tuple-element.6, f32[512]{0:T(512)S(1)} %get-tuple-element.7), kind=kLoop, calls=%fused_computation.8 | loop fusion | flops 37748736 | bytes 8409088 | tf_op jit(solution)/shard_map/convert.1
  64.5 16.3 %all-to-all-done = bf16[4,512,2,128]{3,2,0,1:T(2,128)(2,1)S(1)} async-done(((bf16[4,512,2,128]{3,2,0,1:T(2,128)(2,1)}), bf16[4,512,2,128]{3,2,0,1:T(2,128)(2,1)S(1)}, u32[]{:S(2)}, u32[]{:S(2)}) %all-to-all-start) | async-done | bytes 1048608 | tf_op jit(solution)/shard_map/all_to_all | solution.py:51
  80.9 0.3 copy.21
  81.1 0.0 copy-start.4
  81.1 0.0 copy-start.5
  81.2 0.0 copy-start.7
  81.2 0.0 copy-start.1
  81.2 6.8 %fusion.8 = f32[4,1024]{1,0:T(4,128)S(1)} fusion(bf16[4,1024,128]{1,2,0:T(8,128)(2,1)} %copy.18, bf16[512,4,2,128]{3,0,2,1:T(8,128)(2,1)S(1)} %bitcast.65, bf16[4,1024,1,512]{3,1,2,0:T(8,128)(2,1)} %get-tuple-element.5, bf16[4,1024,1,512]{3,1,2,0:T(8,128)(2,1)} %get-tuple-element.4), kind=kOutput, calls=%fused_computation.18 | convolution fusion | flops 1079504896 | bytes 10502144 | tf_op jit(solution)/shard_map/jqrm,mjrl->jql/dot_general | solution.py:48
  88.0 17.2 %psum.7 = f32[4,1024]{1,0:T(4,128)S(1)} all-reduce(f32[4,1024]{1,0:T(4,128)S(1)} %fusion.8), channel_id=1, replica_groups=mesh['section'=4,'band'=128] {'section'}, use_global_device_ids=true, to_apply=%region_1.2 | all-reduce | flops 4096 | bytes 32768 | tf_op jit(solution)/shard_map/psum | solution.py:55
  105.2 0.0 copy-done.4
  105.2 0.0 copy-done.5
  105.2 0.0 copy-done.7
  105.2 0.7 fusion.47
  105.9 0.0 copy-done.1
  105.9 5.7 %fusion.22 = bf16[512,4,2,128]{0,3,2,1:T(8,128)(2,1)} fusion(bf16[4,1024,1,512]{3,1,2,0:T(8,128)(2,1)} %get-tuple-element.5, bf16[4,1024,1,512]{3,1,2,0:T(8,128)(2,1)} %get-tuple-element.4, bf16[4,1024,128]{1,2,0:T(8,128)(2,1)S(1)} %copy-done.1, f32[4,1024]{1,0:T(4,128)S(1)} %get-tuple-element.2), kind=kOutput, calls=%fused_computation.30 | convolution fusion | flops 1092616192 | bytes 10502144 | tf_op jit(solution)/shard_map/jqrm,jql->mjrl/dot_general | solution.py:28
  111.6 0.0 copy-start.2
  111.6 0.0 copy-start.6
  111.6 2.5 %copy.23 = bf16[512,4,2,128]{3,2,1,0:T(2,128)(2,1)S(1)} copy(bf16[512,4,2,128]{0,3,2,1:T(8,128)(2,1)} %fusion.22) | data formatting | bytes 2097152 | tf_op jit(solution)/shard_map/convert_element_type | solution.py:31
  114.1 61.9 %all_to_all.36 = bf16[512,4,2,128]{3,2,1,0:T(2,128)(2,1)S(1)} all-to-all(bf16[512,4,2,128]{3,2,1,0:T(2,128)(2,1)S(1)} %copy.23), channel_id=1, replica_groups=mesh['section'=4,'band'=128] {'band'}, dimensions={0} | all-to-all | bytes 2097152 | tf_op jit(solution)/shard_map/all_to_all | solution.py:61
  176.0 0.1 copy.24
  176.1 0.8 copy.25
  176.9 0.0 copy-done.2
  176.9 0.0 copy-done.6
  176.9 3.4 %fusion.28 = bf16[1,4,2,128,512]{4,3,2,1,0:T(8,128)(2,1)} fusion(bf16[4,512,512]{2,1,0:T(8,128)(2,1)S(1)} %copy-done, bf16[4,512,2,128]{3,1,2,0:T(8,128)(2,1)S(1)} %bitcast.62, bf16[1,4,2,128,512]{4,3,2,1,0:T(8,128)(2,1)} %param.9, f32[512]{0:T(512)S(1)} %bitcast.67, bf16[1,128,128]{2,1,0:T(8,128)(2,1)S(1)} %copy-done.2), kind=kOutput, calls=%fused_computation.32 | convolution fusion | flops 673710080 | bytes 5277696 | tf_op jit(solution)/shard_map/mjrk,mnj->mrkn/dot_general | solution.py:65
  (1 shorter events, 0.0 us)
Async XLA Ops:
  0.6 1.6 copy-start
  4.5 23.4 %copy-start.3 = (s32[4,1024]{1,0:T(4,128)S(1)}, s32[4,1024]{1,0:T(4,128)}, u32[]{:S(2)}) copy-start(s32[4,1024]{1,0:T(4,128)} %param.13) | copy-start | bytes 49156
  6.6 74.3 %all-to-all-start = ((bf16[4,512,2,128]{3,2,0,1:T(2,128)(2,1)}), bf16[4,512,2,128]{3,2,0,1:T(2,128)(2,1)S(1)}, u32[]{:S(2)}, u32[]{:S(2)}) async-start(bf16[4,512,2,128]{3,2,0,1:T(2,128)(2,1)} %copy.20), calls=%async_computation | async-start | bytes 2097152 | tf_op jit(solution)/shard_map/all_to_all | solution.py:51
  81.1 24.1 %copy-start.4 = (f32[4,1024]{1,0:T(4,128)S(1)}, f32[4,1024]{1,0:T(4,128)}, u32[]{:S(2)}) copy-start(f32[4,1024]{1,0:T(4,128)} %param.17) | copy-start | bytes 49156
  81.1 24.1 %copy-start.5 = (f32[4,1024]{1,0:T(4,128)S(1)}, f32[4,1024]{1,0:T(4,128)}, u32[]{:S(2)}) copy-start(f32[4,1024]{1,0:T(4,128)} %param.16) | copy-start | bytes 49156
  81.2 24.0 %copy-start.7 = (s32[4]{0:T(128)S(1)}, s32[4]{0:T(128)}, u32[]{:S(2)}) copy-start(s32[4]{0:T(128)} %param.14) | copy-start | bytes 52
  81.2 24.7 %copy-start.1 = (bf16[4,1024,128]{1,2,0:T(8,128)(2,1)S(1)}, bf16[4,1024,128]{1,2,0:T(8,128)(2,1)}, u32[]{:S(2)}) copy-start(bf16[4,1024,128]{1,2,0:T(8,128)(2,1)} %copy.18) | copy-start | bytes 3145732
  111.6 65.3 %copy-start.2 = (bf16[1,128,128]{2,1,0:T(8,128)(2,1)S(1)}, bf16[1,128,128]{2,1,0:T(8,128)(2,1)}, u32[]{:S(2)}) copy-start(bf16[1,128,128]{2,1,0:T(8,128)(2,1)} %param.12) | copy-start | bytes 98308
  111.6 65.3 %copy-start.6 = (f32[1,512]{1,0:T(1,128)S(1)}, f32[1,512]{1,0:T(1,128)}, u32[]{:S(2)}) copy-start(f32[1,512]{1,0:T(1,128)} %param.11) | copy-start | bytes 6148
where the time goes:
time: 181 us; the launch traced here: 180 us
  blocking collectives  79 us (44%)
  other arithmetic  37.3 us (21%)
  starting transfers between devices  19 us (10%)
  matrix products  18.2 us (10%)
  waiting for transfers between devices  16.3 us (9%)
  local copies, waits for them, and re-layouts  9.71 us (5%)
    all_to_all x1, blocking collectives, local(): lax.all_to_all(adjoint_fields, 'band', split_axis=0, concat_axis=1, tiled...  61.9 us
    another operation x1, other arithmetic  36.7 us
    all_to_all x1, starting transfers between devices, local(): lax.all_to_all(fields, 'band', split_axis=1, concat_axis=0, tiled=True)  19 us
    psum x1, blocking collectives, local(): evolved = lax.psum(partial_obs, 'section')  17.2 us
    all_to_all x1, waiting for transfers between devices, local(): lax.all_to_all(fields, 'band', split_axis=1, concat_axis=0, tiled=True)  16.3 us
    dot_general x1, matrix products, local(): jnp.einsum('jqrm,mjrl->jql', fourier, lax.all_to_all(fields, 'band', spli...  6.85 us
    dot_general x1, matrix products, observe(): jnp.einsum('jqrm,jql->mjrl', fourier, adjoint_columns, preferred_element_...  5.73 us
    unnamed x17, local copies, waits for them, and re-layouts  3.9 us
  transfers between devices with their start and end apart: 1, of which 1 were waited for; matrix products, arithmetic and copies ran while one was open for 22% of the time, Pallas kernels for 0%

commit v1 on v0

v1 whole, which is shorter than its diff:
```python
import math

import jax
import jax.numpy as jnp
from jax import lax
from jax.sharding import PartitionSpec as P

NLON = 1024
COARSE = 32


def turn(index):
    angle = (index & (NLON - 1)).astype(jnp.float32) * (2.0 * math.pi / NLON)
    return jnp.cos(angle), jnp.sin(angle)


def make_basis(longitude, waves):
    lon = longitude[None, :]
    fine = lax.broadcasted_iota(jnp.int32, (COARSE, 1), 0)
    coarse = lax.broadcasted_iota(jnp.int32, (waves // COARSE, 1), 0) * COARSE
    tables = turn(coarse * lon) + turn(fine * lon)
    cos_a, sin_a, cos_b, sin_b = lax.optimization_barrier(tables)
    cos_a, sin_a = 2.0 * cos_a[:, None, :], 2.0 * sin_a[:, None, :]
    cos_b, sin_b = cos_b[None], sin_b[None]
    wave_ids = lax.broadcasted_iota(jnp.int32, (waves // COARSE, COARSE, 1), 0) * COARSE
    wave_ids = wave_ids + lax.broadcasted_iota(jnp.int32, wave_ids.shape, 1)
    cos_m = jnp.where(wave_ids == 0, 1.0, cos_a * cos_b - sin_a * sin_b)
    sin_m = -(sin_a * cos_b + cos_a * sin_b)
    shape = (waves, longitude.shape[0])
    return cos_m.reshape(shape).astype(jnp.bfloat16), sin_m.reshape(shape).astype(jnp.bfloat16)


def make_local(sections, bands):
    def local(
        control, legendre, spectral_sd, vertical, obs_lon, obs_count, kernels, obs_value, obs_weight
    ):
        coeffs = control[0]
        spread = spectral_sd[0]
        mixing = vertical[0]
        waves_here, _, latitudes = legendre.shape
        levels = mixing.shape[0]
        waves = waves_here * bands
        here = lax.axis_index("section")
        longitude = lax.dynamic_index_in_dim(obs_lon, here, 0, keepdims=False)
        cos_m, sin_m = make_basis(longitude, waves)

        scaled = (coeffs.astype(jnp.float32) * spread).astype(jnp.bfloat16)
        spectral_rows = jnp.einsum(
            "mnj,mrkn->mjrk", legendre, scaled, preferred_element_type=jnp.float32
        ).astype(jnp.bfloat16)
        fields = jnp.einsum(
            "mjrk,lk->mjrl", spectral_rows, mixing, preferred_element_type=jnp.float32
        ).astype(jnp.bfloat16)
        fields = fields.reshape(waves_here, bands, sections, 2, levels).transpose(2, 1, 0, 3, 4)
        shares = lax.all_to_all(fields, "section", split_axis=0, concat_axis=0, tiled=True)
        field_sum = jnp.sum(shares.astype(jnp.float32), axis=0).astype(jnp.bfloat16)
        row_fields = lax.all_to_all(field_sum, "band", split_axis=0, concat_axis=0, tiled=True)
        row_fields = row_fields.reshape(waves, 2, levels)

        kern = lax.dynamic_index_in_dim(kernels, here, 0, keepdims=False)
        value = lax.dynamic_index_in_dim(obs_value, here, 0, keepdims=False)
        weight = lax.dynamic_index_in_dim(obs_weight, here, 0, keepdims=False)
        count = lax.dynamic_index_in_dim(obs_count, here, 0, keepdims=False)
        columns = jnp.einsum(
            "mq,ml->ql", cos_m, row_fields[:, 0], preferred_element_type=jnp.float32
        ) + jnp.einsum("mq,ml->ql", sin_m, row_fields[:, 1], preferred_element_type=jnp.float32)
        evolved = jnp.sum(kern.astype(jnp.float32) * columns, axis=-1)
        is_live = lax.broadcasted_iota(jnp.int32, evolved.shape, 0) < count
        departures = jnp.where(is_live, evolved - value, jnp.float32(0.0))
        adjoint_columns = ((weight * departures)[:, None] * kern.astype(jnp.float32)).astype(
            jnp.bfloat16
        )
        adjoint = [
            jnp.einsum("mq,ql->ml", basis, adjoint_columns, preferred_element_type=jnp.float32)
            for basis in (cos_m, sin_m)
        ]
        adjoint = jnp.stack(adjoint, axis=1).astype(jnp.bfloat16)
        adjoint = adjoint.reshape(bands, waves_here, 2, levels)
        back = lax.all_to_all(adjoint, "band", split_axis=0, concat_axis=0, tiled=True)
        piece1 = departures.astype(jnp.bfloat16)
        rest = departures - piece1.astype(jnp.float32)
        piece2 = rest.astype(jnp.bfloat16)
        piece3 = (rest - piece2.astype(jnp.float32)).astype(jnp.bfloat16)
        pieces = jnp.concatenate([piece1, piece2, piece3]).reshape(-1, levels)
        packet = jnp.concatenate([back.reshape(-1, levels), pieces], axis=0)
        packets = lax.all_to_all(
            jnp.broadcast_to(packet[None], (sections,) + packet.shape),
            "section", split_axis=0, concat_axis=0, tiled=True,
        )
        body = bands * waves_here * 2
        back_all = packets[:, :body].reshape(sections, bands, waves_here, 2, levels)
        parts = packets[:, body:].astype(jnp.float32).reshape(sections, 3, -1)
        all_departures = (parts[:, 2] + parts[:, 1]) + parts[:, 0]

        back_rows = jnp.einsum(
            "tbmrl,lk->tbmrk", back_all, mixing, preferred_element_type=jnp.float32
        ).astype(jnp.bfloat16)
        basis_rows = legendre.reshape(waves_here, -1, bands, sections)
        gradient_terms = jnp.einsum(
            "tbmrk,mnbt->mrkn", back_rows, basis_rows, preferred_element_type=jnp.float32
        )
        gradient = (coeffs.astype(jnp.float32) + spread * gradient_terms).astype(jnp.bfloat16)
        return (gradient[None], all_departures)

    return local


def solution(mesh):
    in_specs = (
        P("section", "band", None, None, None),
        P("band", None, None),
        P("section", None),
        P("section", None, None),
        P("band", None),
        P("band"),
        P("band", None, None),
        P("band", None),
        P("band", None),
    )
    out_specs = (P("section", "band", None, None, None), P("band", None))
    local = make_local(mesh.shape["section"], mesh.shape["band"])
    return jax.shard_map(local, mesh=mesh, in_specs=in_specs, out_specs=out_specs, check_vma=False)
```

time: 181 us -> 131 us (0.72)
  blocking collectives: 79 us -> 0 us
  waiting for transfers between devices: 16.3 us -> 52.7 us
  other arithmetic: 37.3 us -> 8.36 us
  starting transfers between devices: 19 us -> 33.7 us
  local copies, waits for them, and re-layouts: 9.71 us -> 23 us
  matrix products: 18.2 us -> 12.1 us
    all_to_all x1 -> x0, blocking collectives: 61.9 us -> none  [local(): lax.all_to_all(adjoint_fields, 'band', split_axis=0, concat_axis=1, tiled...]
    another operation x1, other arithmetic: 36.7 us -> 0.03 us  [local(): adjoint = jnp.stack(adjoint, axis=1).astype(jnp.bfloat16)]
    all_to_all x1 -> x4, waiting for transfers between devices: 16.3 us -> 52.7 us  [the longest x1 21.8 us: local(): lax.all_to_all(adjoint, 'band', split_axis=0, concat_axis=0, tiled=True)]
    psum x1 -> x0, blocking collectives: 17.2 us -> none  [local(): evolved = lax.psum(partial_obs, 'section')]
    all_to_all x1 -> x4, starting transfers between devices: 19 us -> 33.7 us  [the longest x1 19.5 us: local(): lax.all_to_all(field_sum, 'band', split_axis=0, concat_axis=0, tiled=True)]
    dot_general x3 -> x5, matrix products: 16 us -> 9.05 us  [the longest x1 5.72 us: local(): jnp.einsum('tbmrk,mnbt->mrkn', back_rows, basis_rows, preferred_element_t...]
    mul x0 -> x6, local copies, waits for them, and re-layouts: none -> 4.76 us  [make_basis(): cos_m = jnp.where(wave_ids == 0, 1.0, cos_a * cos_b - sin_a * sin_b)]
    convert_element_type x0 -> x3, other arithmetic: none -> 4.61 us  [the longest x1 3.95 us: make_basis(): cos_m.reshape(shape).astype(jnp.bfloat16)]
  transfers between devices with their start and end apart: 1 -> 4, of which waited for: 1 -> 4; matrix products, arithmetic and copies ran while one was open for 22% -> 18% of each run, Pallas kernels for 0% -> 0%
where the time goes in v1:
time: 131 us
  waiting for transfers between devices  52.7 us (40%)
  starting transfers between devices  33.7 us (26%)
  local copies, waits for them, and re-layouts  23 us (18%)
  matrix products  12.1 us (9%)
  other arithmetic  8.36 us (6%)
    all_to_all x1, waiting for transfers between devices, local(): lax.all_to_all(adjoint, 'band', split_axis=0, concat_axis=0, tiled=True)  21.8 us
    all_to_all x1, starting transfers between devices, local(): lax.all_to_all(field_sum, 'band', split_axis=0, concat_axis=0, tiled=True)  19.5 us
    all_to_all x1, waiting for transfers between devices, local(): lax.all_to_all(jnp.broadcast_to(packet[None], (sections,) + packet.shape)...  11.4 us
    all_to_all x1, waiting for transfers between devices, local(): lax.all_to_all(field_sum, 'band', split_axis=0, concat_axis=0, tiled=True)  11.3 us
    all_to_all x1, waiting for transfers between devices, local(): lax.all_to_all(fields, 'section', split_axis=0, concat_axis=0, tiled=True)  8.19 us
    unnamed x21, local copies, waits for them, and re-layouts  6.28 us
    all_to_all x1, starting transfers between devices, local(): lax.all_to_all(adjoint, 'band', split_axis=0, concat_axis=0, tiled=True)  6.27 us
    dot_general x1, matrix products, local(): jnp.einsum('tbmrk,mnbt->mrkn', back_rows, basis_rows, preferred_element_t...  5.72 us
  transfers between devices with their start and end apart: 4, of which 4 were waited for; matrix products, arithmetic and copies ran while one was open for 18% of the time, Pallas kernels for 0%

profile of v1, /device:TPU:32, one launch (start us, length us, event | category | flops | bytes accessed | tf_op | source)
XLA Modules:
  0.0 130.8 jit_solution(1249564889309278482)
XLA Ops:
  0.6 0.0 copy-start
  0.6 3.0 %convolution_convert_fusion.1 = bf16[4,512,2,128]{3,1,2,0:T(8,128)(2,1)S(1)} fusion(bf16[4,512,512]{2,1,0:T(8,128)(2,1)} %param.10, bf16[1,4,2,128,512]{4,3,2,1,0:T(8,128)(2,1)} %param.9, f32[512]{0:T(512)} %bitcast.113, bf16[1,128,128]{2,1,0:T(8,128)(2,1)} %param.12), kind=kOutput, calls=%fused_computation.15 | convolution fusion | flops 673710080 | bytes 4229120 | tf_op jit(solution)/shard_map/mjrk,lk->mjrl/dot_general | solution.py:51
  3.6 1.2 copy.85
  4.9 4.5 %all-to-all-start = ((bf16[4,128,4,2,128]{4,1,3,2,0:T(8,128)(2,1)}), bf16[4,128,4,2,128]{4,1,3,2,0:T(8,128)(2,1)}, u32[]{:S(2)}, u32[]{:S(2)}) async-start(bf16[4,128,4,2,128]{4,1,3,2,0:T(8,128)(2,1)} %bitcast.97), calls=%async_computation | async-start | bytes 2097152 | tf_op jit(solution)/shard_map/all_to_all | solution.py:55
  9.3 0.7 constant_dynamic-slice_fusion.3
  10.1 1.2 fusion.38
  11.2 0.3 fusion.40
  11.6 0.6 mul.251
  12.2 1.7 %mul.252 = f32[16,32,1024]{2,1,0:T(8,128)} reshape(f32[128,4,1024]{2,1,0:T(4,128)S(1)} %mul.251) | data formatting | bytes 4194304 | tf_op jit(solution)/shard_map/mul | solution.py:27
  14.0 0.6 mul.258
  14.6 1.7 %mul.259 = f32[16,32,1024]{2,1,0:T(8,128)} reshape(f32[128,4,1024]{2,1,0:T(4,128)S(1)} %mul.258) | data formatting | bytes 4194304 | tf_op jit(solution)/shard_map/mul | solution.py:27
  16.4 0.0 copy-start.8
  16.4 0.0 copy-start.1
  16.4 8.2 %all-to-all-done = bf16[4,128,4,2,128]{4,1,3,2,0:T(8,128)(2,1)} async-done(((bf16[4,128,4,2,128]{4,1,3,2,0:T(8,128)(2,1)}), bf16[4,128,4,2,128]{4,1,3,2,0:T(8,128)(2,1)}, u32[]{:S(2)}, u32[]{:S(2)}) %all-to-all-start) | async-done | bytes 1048608 | tf_op jit(solution)/shard_map/all_to_all | solution.py:55
  24.6 1.4 %reduce_sum.23 = bf16[128,4,2,128]{3,0,2,1:T(8,128)(2,1)S(1)} reduce(bf16[4,128,4,2,128]{4,1,3,2,0:T(8,128)(2,1)} %all-to-all-done, bf16[]{:T(256)} %constant.46.clone.1), dimensions={0}, to_apply=%region_0.1 | reduce | flops 393216 | bytes 1310722 | tf_op jit(solution)/shard_map/reduce_sum | solution.py:56
  26.0 0.9 copy.42
  26.9 19.5 %all-to-all-start.1 = ((bf16[128,4,2,128]{3,1,2,0:T(4,128)(2,1)}), bf16[128,4,2,128]{3,1,2,0:T(4,128)(2,1)}, u32[]{:S(2)}, u32[]{:S(2)}) async-start(bf16[128,4,2,128]{3,1,2,0:T(4,128)(2,1)} %copy.42), calls=%async_computation.1 | async-start | bytes 524288 | tf_op jit(solution)/shard_map/all_to_all | solution.py:57
  46.4 0.1 iota.75
  46.5 0.0 copy-done
  46.5 0.7 constant_dynamic-slice_fusion.1
  47.2 1.1 copy.69
  48.3 0.0 copy-done.8
  48.3 0.6 dynamic_slice.21
  48.9 0.1 add_compare_fusion.1
  48.9 0.0 copy-done.1
  49.0 4.0 %select_convert_fusion.1 = (bf16[16,32,1024]{2,1,0:T(8,128)(2,1)}, bf16[16,32,1024]{2,1,0:T(8,128)(2,1)}, bf16[16,32,1024]{2,1,0:T(8,128)(2,1)}, bf16[16,32,1024]{2,1,0:T(8,128)(2,1)}) fusion(f32[16,32,1024]{2,1,0:T(8,128)} %mul.259, f32[16,32,1024]{2,1,0:T(8,128)S(1)} %copy-done.1, f32[32,1024]{1,0:T(8,128)} %get-tuple-element.9, ...), kind=kLoop, calls=%fused_computation.12 | loop fusion | flops 10485760 | bytes 8782848 | tf_op jit(solution)/shard_map/convert_element_type | solution.py:30
  52.9 0.0 copy-start.2
  52.9 2.3 %convert_element_type.131 = bf16[128,4,1024]{2,1,0:T(4,128)(2,1)} reshape(bf16[16,32,1024]{2,1,0:T(8,128)(2,1)} %get-tuple-element.12) | data formatting | bytes 2097152 | tf_op jit(solution)/shard_map/convert_element_type | solution.py:30
  55.2 0.0 copy-done.2
  55.2 0.0 copy-start.3
  55.2 1.2 convert_element_type.146
  56.4 0.7 constant_dynamic-slice_fusion
  57.2 11.3 %all-to-all-done.1 = bf16[128,4,2,128]{3,1,2,0:T(4,128)(2,1)} async-done(((bf16[128,4,2,128]{3,1,2,0:T(4,128)(2,1)}), bf16[128,4,2,128]{3,1,2,0:T(4,128)(2,1)}, u32[]{:S(2)}, u32[]{:S(2)}) %all-to-all-start.1) | async-done | bytes 262176 | tf_op jit(solution)/shard_map/all_to_all | solution.py:57
  68.5 0.0 copy-start.5
  68.5 1.1 copy.43
  69.6 1.6 %fusion.37 = f32[1024,128]{0,1:T(8,128)S(1)} fusion(bf16[512,1024]{1,0:T(8,128)(2,1)} %bitcast.100, bf16[512,2,128]{2,0,1:T(8,128)(2,1)S(1)} %bitcast.105), kind=kOutput, calls=%fused_computation.41 | convolution fusion | flops 134217728 | bytes 1703936 | tf_op jit(solution)/shard_map/mq,ml->ql/dot_general | solution.py:64
  71.2 0.0 copy-start.4
  71.2 0.0 copy-done.3
  71.3 0.4 fusion.20
  71.6 0.7 select_multiply_fusion
  72.3 0.0 copy-done.5
  72.3 0.7 fusion.21
  73.0 0.0 copy-done.4
  73.0 0.7 fusion.22
  73.7 0.9 copy.48
  74.7 6.3 %all-to-all-start.2 = ((bf16[128,4,2,128]{3,1,2,0:T(4,128)(2,1)}), bf16[128,4,2,128]{3,1,2,0:T(4,128)(2,1)S(1)}, u32[]{:S(2)}, u32[]{:S(2)}) async-start(bf16[128,4,2,128]{3,1,2,0:T(4,128)(2,1)} %copy.48), calls=%async_computation.2 | async-start | bytes 524288 | tf_op jit(solution)/shard_map/all_to_all | solution.py:79
  80.9 0.7 fusion.47
  81.6 21.8 %all-to-all-done.2 = bf16[128,4,2,128]{3,1,2,0:T(4,128)(2,1)S(1)} async-done(((bf16[128,4,2,128]{3,1,2,0:T(4,128)(2,1)}), bf16[128,4,2,128]{3,1,2,0:T(4,128)(2,1)S(1)}, u32[]{:S(2)}, u32[]{:S(2)}) %all-to-all-start.2) | async-done | bytes 262176 | tf_op jit(solution)/shard_map/all_to_all | solution.py:79
  103.4 0.2 copy.49
  103.7 1.1 broadcast_in_dim.40
  104.8 3.5 %all-to-all-start.3 = ((bf16[4,1048,128]{2,1,0:T(8,128)(2,1)}), bf16[4,1048,128]{2,1,0:T(8,128)(2,1)S(1)}, u32[]{:S(2)}, u32[]{:S(2)}) async-start(bf16[4,1048,128]{2,1,0:T(8,128)(2,1)} %broadcast_in_dim.40), calls=%async_computation.3 | async-start | bytes 2146304 | tf_op jit(solution)/shard_map/all_to_all | solution.py:86
  108.3 4.5 %copy.51 = bf16[4,512,512]{1,0,2:T(4,128)(2,1)} copy(bf16[4,512,512]{2,1,0:T(8,128)(2,1)} %param.10) | data formatting | bytes 4194304 | tf_op args[1]
  112.9 0.0 copy-start.6
  112.9 0.0 copy-start.7
  112.9 11.4 %all-to-all-done.3 = bf16[4,1048,128]{2,1,0:T(8,128)(2,1)S(1)} async-done(((bf16[4,1048,128]{2,1,0:T(8,128)(2,1)}), bf16[4,1048,128]{2,1,0:T(8,128)(2,1)S(1)}, u32[]{:S(2)}, u32[]{:S(2)}) %all-to-all-start.3) | async-done | bytes 1073184 | tf_op jit(solution)/shard_map/all_to_all | solution.py:86
  124.3 0.6 copy.86
  125.0 0.1 slice.30
  125.0 0.0 copy-done.6
  125.0 0.0 copy-done.7
  125.0 5.7 %fusion.16 = bf16[1,4,2,128,512]{4,3,2,1,0:T(8,128)(2,1)} fusion(bf16[4,512,128,4,1]{1,0,3,2,4:T(4,128)(2,1)} %bitcast.101, bf16[1,4,2,128,512]{4,3,2,1,0:T(8,128)(2,1)} %param.9, bf16[4,128,4,2,128]{4,3,2,1,0:T(2,128)(2,1)S(1)} %bitcast.102, f32[512]{0:T(512)S(1)} %bitcast.114, bf16[1,128,128]{2,1,0:T(8,128)(2,1)S(1)} %copy-done.6), kind=kOutput, calls=%fused_computation.17 | convolution fusion | flops 673710080 | bytes 5277696 | tf_op jit(solution)/shard_map/tbmrk,mnbt->mrkn/dot_general | solution.py:99
  (11 shorter events, 0.2 us)
Async XLA Ops:
  0.6 45.8 %copy-start = (bf16[4,1024,128]{2,1,0:T(8,128)(2,1)S(1)}, bf16[4,1024,128]{2,1,0:T(8,128)(2,1)}, u32[]{:S(2)}) copy-start(bf16[4,1024,128]{2,1,0:T(8,128)(2,1)} %param.15) | copy-start | bytes 3145732
  4.9 19.7 %all-to-all-start = ((bf16[4,128,4,2,128]{4,1,3,2,0:T(8,128)(2,1)}), bf16[4,128,4,2,128]{4,1,3,2,0:T(8,128)(2,1)}, u32[]{:S(2)}, u32[]{:S(2)}) async-start(bf16[4,128,4,2,128]{4,1,3,2,0:T(8,128)(2,1)} %bitcast.97), calls=%async_computation | async-start | bytes 2097152 | tf_op jit(solution)/shard_map/all_to_all | solution.py:55
  16.4 31.9 %copy-start.8 = (s32[4]{0:T(128)S(1)}, s32[4]{0:T(128)}, u32[]{:S(2)}) copy-start(s32[4]{0:T(128)} %param.14) | copy-start | bytes 52
  16.4 32.6 %copy-start.1 = (f32[16,32,1024]{2,1,0:T(8,128)S(1)}, f32[16,32,1024]{2,1,0:T(8,128)}, u32[]{:S(2)}) copy-start(f32[16,32,1024]{2,1,0:T(8,128)} %mul.252) | copy-start | bytes 6291460
  26.9 41.6 %all-to-all-start.1 = ((bf16[128,4,2,128]{3,1,2,0:T(4,128)(2,1)}), bf16[128,4,2,128]{3,1,2,0:T(4,128)(2,1)}, u32[]{:S(2)}, u32[]{:S(2)}) async-start(bf16[128,4,2,128]{3,1,2,0:T(4,128)(2,1)} %copy.42), calls=%async_computation.1 | async-start | bytes 524288 | tf_op jit(solution)/shard_map/all_to_all | solution.py:57
  52.9 2.3 %copy-start.2 = (bf16[16,32,1024]{2,1,0:T(8,128)(2,1)S(1)}, bf16[16,32,1024]{2,1,0:T(8,128)(2,1)}, u32[]{:S(2)}) copy-start(bf16[16,32,1024]{2,1,0:T(8,128)(2,1)} %get-tuple-element.13) | copy-start | bytes 3145732
  55.2 16.0 %copy-start.3 = (bf16[16,32,1024]{2,1,0:T(8,128)(2,1)S(1)}, bf16[16,32,1024]{2,1,0:T(8,128)(2,1)}, u32[]{:S(2)}) copy-start(bf16[16,32,1024]{2,1,0:T(8,128)(2,1)} %get-tuple-element.17) | copy-start | bytes 3145732
  68.5 3.8 %copy-start.5 = (bf16[128,4,1024]{2,1,0:T(4,128)(2,1)S(1)}, bf16[128,4,1024]{2,1,0:T(4,128)(2,1)}, u32[]{:S(2)}) copy-start(bf16[128,4,1024]{2,1,0:T(4,128)(2,1)} %convert_element_type.131) | copy-start | bytes 3145732
  71.2 1.8 %copy-start.4 = (bf16[128,4,1024]{2,1,0:T(4,128)(2,1)S(1)}, bf16[128,4,1024]{2,1,0:T(4,128)(2,1)}, u32[]{:S(2)}) copy-start(bf16[128,4,1024]{2,1,0:T(4,128)(2,1)} %convert_element_type.146) | copy-start | bytes 3145732
  74.7 28.8 %all-to-all-start.2 = ((bf16[128,4,2,128]{3,1,2,0:T(4,128)(2,1)}), bf16[128,4,2,128]{3,1,2,0:T(4,128)(2,1)S(1)}, u32[]{:S(2)}, u32[]{:S(2)}) async-start(bf16[128,4,2,128]{3,1,2,0:T(4,128)(2,1)} %copy.48), calls=%async_computation.2 | async-start | bytes 524288 | tf_op jit(solution)/shard_map/all_to_all | solution.py:79
  104.8 19.5 %all-to-all-start.3 = ((bf16[4,1048,128]{2,1,0:T(8,128)(2,1)}), bf16[4,1048,128]{2,1,0:T(8,128)(2,1)S(1)}, u32[]{:S(2)}, u32[]{:S(2)}) async-start(bf16[4,1048,128]{2,1,0:T(8,128)(2,1)} %broadcast_in_dim.40), calls=%async_computation.3 | async-start | bytes 2146304 | tf_op jit(solution)/shard_map/all_to_all | solution.py:86
  112.9 12.2 %copy-start.6 = (bf16[1,128,128]{2,1,0:T(8,128)(2,1)S(1)}, bf16[1,128,128]{2,1,0:T(8,128)(2,1)}, u32[]{:S(2)}) copy-start(bf16[1,128,128]{2,1,0:T(8,128)(2,1)} %param.12) | copy-start | bytes 98308
  112.9 12.2 %copy-start.7 = (f32[1,512]{1,0:T(1,128)S(1)}, f32[1,512]{1,0:T(1,128)}, u32[]{:S(2)}) copy-start(f32[1,512]{1,0:T(1,128)} %param.11) | copy-start | bytes 6148

commit v2 on v0

v2 whole, which is shorter than its diff:
```python
import functools
import math

import jax
import jax.numpy as jnp
from jax import lax
from jax.experimental import pallas as pl
from jax.experimental.pallas import tpu as pltpu
from jax.sharding import PartitionSpec as P

NLON = 1024
FINE = 64
F32 = jnp.float32
BF16 = jnp.bfloat16
MINOR_BOTH = (((1,), (1,)), ((), ()))


WHOLE = pl.BlockSpec(memory_space=pltpu.VMEM)
SCALAR = pl.BlockSpec(memory_space=pltpu.SMEM)
APART = pl.BlockSpec(memory_space=pl.ANY)


LIMIT = pltpu.CompilerParams(vmem_limit_bytes=16 << 20)


def made(shape, kind):
    return pltpu.VMEM(shape, kind)


def near(array):
    return pltpu.with_memory_space_constraint(array, pltpu.VMEM)


def view(ref, shape):
    return ref.reshape(shape)


def far(array):
    return pltpu.with_memory_space_constraint(array, pltpu.HBM)


def dot(a, b):
    return jnp.dot(a, b, preferred_element_type=F32)


def dot_minor(a, b):
    return lax.dot_general(a, b, MINOR_BOTH, preferred_element_type=F32)


def grouping(sections, bands):
    size = sections * bands
    shift = bands.bit_length() - 1
    place = lax.broadcasted_iota(jnp.int32, (size, size), 0)
    row = lax.broadcasted_iota(jnp.int32, (size, size), 1)
    home = sections * (place & (bands - 1)) + lax.shift_right_logical(place, shift)
    return jnp.where(home == row, 1.0, 0.0).astype(BF16)


def pull(pairs, sems):
    copies = [pltpu.make_async_copy(a, b, sems.at[i]) for i, (a, b) in enumerate(pairs)]
    for copy in copies:
        copy.start()
    return copies


def forward_body(
    sections, bands, control, legendre, spread, mixing, out,
    held, coeffs, basis, spreads, mixings, diagonal, sems,
):
    waves_here, pairs, _ = control.shape
    levels = mixing.shape[0]
    latitudes = legendre.shape[2]
    tile = 2 * waves_here
    order = [(spread, spreads), (mixing, mixings)]
    for m in range(waves_here):
        order += [(control.at[m], coeffs.at[m]), (legendre.at[m], basis.at[m])]
    copies = pull(order, sems)
    copies[0].wait()
    copies[1].wait()
    diagonal[...] = jnp.zeros_like(diagonal)
    for r in range(2):
        part = pl.ds(r * levels, levels)
        diagonal[part, part] = mixings[...]
    for m in range(waves_here):
        copies[2 + 2 * m].wait()
        copies[3 + 2 * m].wait()
        scaled = (coeffs[m].astype(F32) * spreads[...]).astype(BF16)
        rows = lax.dot_general(
            basis[m], scaled, (((0,), (1,)), ((), ())), preferred_element_type=F32
        ).astype(BF16)
        fields = dot_minor(rows, diagonal[...])
        for r in range(2):
            held[pl.ds(2 * m + r, latitudes, stride=tile), :] = fields[
                :, r * levels : (r + 1) * levels
            ]
    placed = view(held, (bands, sections, tile, levels))
    for t in range(sections):
        out[pl.ds(t * bands * tile, bands * tile), :] = (
            placed[:, t].reshape(bands * tile, levels).astype(BF16)
        )


def forward_fields(control, legendre, spread, mixing, sections, bands):
    waves_here, pairs, numbers = control.shape
    latitudes = legendre.shape[2]
    levels = mixing.shape[0]
    rows = latitudes * 2 * waves_here
    return pl.pallas_call(
        functools.partial(forward_body, sections, bands),
        in_specs=[APART] * 4,
        out_specs=WHOLE,
        out_shape=made((rows, levels), BF16),
        scratch_shapes=[
            pltpu.VMEM((rows, levels), F32),
            pltpu.VMEM(control.shape, BF16),
            pltpu.VMEM(legendre.shape, BF16),
            pltpu.VMEM(spread.shape, F32),
            pltpu.VMEM(mixing.shape, BF16),
            pltpu.VMEM((2 * levels, 2 * levels), BF16),
            pltpu.SemaphoreType.DMA((2 + 2 * waves_here,)),
        ],
        name="forward_fields",
        compiler_params=LIMIT,
    )(far(control), far(legendre), far(spread), far(mixing))


def turn(index):
    angle = (index & (NLON - 1)).astype(F32) * (2.0 * math.pi / NLON)
    return jnp.cos(angle), jnp.sin(angle)


def basis_body(here, obs_lon, by_wave):
    terms, _ = by_wave.shape
    lon = obs_lon[pl.ds(here[0], 1), :]
    fine = lax.broadcasted_iota(jnp.int32, (FINE, 1), 0)
    coarse = lax.broadcasted_iota(jnp.int32, (terms // FINE, 1), 0)
    fine_cos, fine_sin = turn(lax.shift_right_logical(fine, 1) * lon + (fine & 1) * (NLON // 4))
    coarse_cos, coarse_sin = turn(coarse * (FINE // 2) * lon)
    coarse_cos, coarse_sin = 2.0 * coarse_cos, 2.0 * coarse_sin
    for a in range(terms // FINE):
        block = coarse_cos[a : a + 1] * fine_cos - coarse_sin[a : a + 1] * fine_sin
        if a == 0:
            block = jnp.where(fine < 2, fine_cos, block)
        by_wave[pl.ds(a * FINE, FINE), :] = block.astype(BF16)


def make_basis(here, obs_lon, terms):
    return pl.pallas_call(
        basis_body,
        in_specs=[SCALAR, WHOLE],
        out_specs=WHOLE,
        out_shape=made((terms, obs_lon.shape[1]), BF16),
        name="make_basis",
        compiler_params=LIMIT,
    )(here, obs_lon)


def observe_body(
    here, count, by_wave, fields, kernels, value, weight, adjoint, pieces, kern, departures, sems
):
    copy = pull([(kernels.at[here[0]], kern)], sems)[0]
    columns = lax.dot_general(
        by_wave[...], fields[...], (((0,), (0,)), ((), ())), preferred_element_type=F32
    )
    slots, lanes = kern.shape
    half = lanes // 2
    line = pl.ds(here[0], 1)
    rows = [jnp.broadcast_to(part[line, :], (half, slots)) for part in (value, weight)]
    known = jnp.concatenate(rows, axis=0).T
    copy.wait()
    wide = kern[...].astype(F32)
    evolved = jnp.sum(wide * columns, axis=1, keepdims=True)
    slot = lax.broadcasted_iota(jnp.int32, evolved.shape, 0)
    departed = jnp.where(slot < count[here[0]], evolved - known[:, :1], 0.0)
    scaled = (known[:, half : half + 1] * departed * wide).astype(BF16)
    adjoint[...] = dot(by_wave[...], scaled).astype(BF16)
    diagonal = lax.broadcasted_iota(jnp.int32, (lanes, lanes), 0) == lax.broadcasted_iota(
        jnp.int32, (lanes, lanes), 1
    )
    for i in range(slots // lanes):
        spot = jnp.where(diagonal, departed[i * lanes : (i + 1) * lanes], 0.0)
        departures[pl.ds(i, 1), :] = jnp.sum(spot, axis=0, keepdims=True)
    rest = departures[...]
    size = rest.shape[0]
    for i in range(3):
        piece = rest.astype(BF16)
        pieces[pl.ds(i * size, size), :] = piece
        rest = rest - piece.astype(F32)


def observe(here, count, by_wave, fields, kernels, value, weight):
    _, slots, levels = kernels.shape
    return pl.pallas_call(
        observe_body,
        in_specs=[SCALAR, SCALAR, WHOLE, WHOLE, APART, WHOLE, WHOLE],
        out_specs=[WHOLE, WHOLE],
        out_shape=[made(fields.shape, BF16), made((3 * slots // levels, levels), BF16)],
        scratch_shapes=[
            pltpu.VMEM((slots, levels), BF16),
            pltpu.VMEM((slots // levels, levels), F32),
            pltpu.SemaphoreType.DMA((1,)),
        ],
        name="observe",
        compiler_params=LIMIT,
    )(here, count, near(by_wave), near(fields), far(kernels), near(value), near(weight))


def sum_body(parts, out):
    total = parts[0].astype(F32)
    for section in range(1, parts.shape[0]):
        total = total + parts[section].astype(F32)
    out[...] = total.astype(BF16)


def sum_sections(parts):
    return pl.pallas_call(
        sum_body,
        in_specs=[WHOLE],
        out_specs=WHOLE,
        out_shape=made(parts.shape[1:], BF16),
        name="sum_sections",
        compiler_params=LIMIT,
    )(near(parts))


def regroup_body(sections, bands, legendre, out):
    group = grouping(sections, bands)
    for m in range(legendre.shape[0]):
        out[m] = dot_minor(legendre[m], group).astype(BF16)


def regroup(legendre, sections, bands):
    return pl.pallas_call(
        functools.partial(regroup_body, sections, bands),
        in_specs=[WHOLE],
        out_specs=WHOLE,
        out_shape=jax.ShapeDtypeStruct(legendre.shape, BF16),
        name="regroup",
        compiler_params=LIMIT,
    )(legendre)


def pack_body(body, pieces, out):
    rows = body.shape[0]
    for section in range(out.shape[0]):
        out[section, pl.ds(0, rows), :] = body[...]
        out[section, pl.ds(rows, pieces.shape[0]), :] = pieces[...]


def pack(body, pieces, sections):
    rows = body.shape[0] + pieces.shape[0]
    return pl.pallas_call(
        pack_body,
        in_specs=[WHOLE, WHOLE],
        out_specs=WHOLE,
        out_shape=made((sections, rows, body.shape[1]), BF16),
        name="pack",
        compiler_params=LIMIT,
    )(near(body), near(pieces))


def backward_body(packets, grouped, control, spread, mixing, out, departures, held, ready, sems):
    sections, _, levels = packets.shape
    waves_here = grouped.shape[0]
    latitudes = grouped.shape[2]
    tile = 2 * waves_here
    size = latitudes // sections * tile
    mixing_t = mixing[...].astype(F32).T.astype(BF16)
    lines = departures.shape[1] // levels
    for t in range(sections):
        held[pl.ds(t * size, size), :] = packets[t, pl.ds(0, size), :].astype(F32)
        parts = [packets[t, pl.ds(size + i * lines, lines), :].astype(F32) for i in range(3)]
        whole = (parts[2] + parts[1]) + parts[0]
        for i in range(lines):
            departures[pl.ds(t, 1), pl.ds(i * levels, levels)] = whole[i : i + 1]
    leaving = []
    for m in range(waves_here):
        rows = [held[pl.ds(2 * m + r, latitudes, stride=tile), :].astype(BF16) for r in range(2)]
        terms = dot(grouped[m], jnp.concatenate(rows, axis=1)).astype(BF16)
        for r in range(2):
            part = pl.ds(r * levels, levels)
            total = dot_minor(mixing_t, terms[:, r * levels : (r + 1) * levels])
            ready[m, part, :] = (control[m, part, :].astype(F32) + spread[...] * total).astype(BF16)
        copy = pltpu.make_async_copy(ready.at[m], out.at[m], sems.at[m])
        copy.start()
        leaving.append(copy)
    for copy in leaving:
        copy.wait()


def backward_gradient(packets, grouped, control, spread, mixing, slots):
    sections, _, levels = packets.shape
    waves_here, _, latitudes = grouped.shape
    return pl.pallas_call(
        backward_body,
        in_specs=[WHOLE] * 5,
        out_specs=[APART, WHOLE],
        out_shape=[
            jax.ShapeDtypeStruct(control.shape, BF16),
            jax.ShapeDtypeStruct((sections, slots), F32),
        ],
        scratch_shapes=[
            pltpu.VMEM((latitudes * 2 * waves_here, levels), F32),
            pltpu.VMEM(control.shape, BF16),
            pltpu.SemaphoreType.DMA((waves_here,)),
        ],
        name="backward_gradient",
        compiler_params=LIMIT,
    )(near(packets), near(grouped), near(control), near(spread), near(mixing))


def make_local(sections, bands):
    def local(
        control, legendre, spectral_sd, vertical, obs_lon, obs_count, kernels, obs_value, obs_weight
    ):
        mixing = vertical[0]
        waves_here, numbers, latitudes = legendre.shape
        levels = mixing.shape[0]
        tile = 2 * waves_here
        terms = tile * bands
        slots = obs_lon.shape[1]
        here = lax.axis_index("section").astype(jnp.int32)
        coeffs = control.reshape(waves_here, 2 * levels, numbers)

        fields = forward_fields(coeffs, legendre, spectral_sd, mixing, sections, bands)
        shares = lax.all_to_all(
            fields.reshape(sections, bands, tile, levels),
            "section", split_axis=0, concat_axis=0, tiled=True,
        )
        field_sum = sum_sections(shares.reshape(sections, terms, levels))
        row_fields = lax.all_to_all(
            field_sum.reshape(bands, tile, levels), "band", split_axis=0, concat_axis=0, tiled=True
        )

        by_wave = make_basis(here[None], obs_lon, terms)
        grouped = regroup(legendre, sections, bands)
        row_fields, by_wave, grouped = lax.optimization_barrier((row_fields, by_wave, grouped))
        adjoint, pieces = observe(
            here[None], obs_count, by_wave, row_fields.reshape(terms, levels),
            kernels, obs_value, obs_weight,
        )
        back = lax.all_to_all(
            adjoint.reshape(bands, tile, levels), "band", split_axis=0, concat_axis=0, tiled=True
        )
        packets = lax.all_to_all(
            pack(back.reshape(terms, levels), pieces, sections),
            "section", split_axis=0, concat_axis=0, tiled=True,
        )
        gradient, all_departures = backward_gradient(
            packets, grouped, coeffs, spectral_sd, mixing, slots
        )
        return (gradient.reshape(control.shape), all_departures)

    return local


def solution(mesh):
    in_specs = (
        P("section", "band", None, None, None),
        P("band", None, None),
        P("section", None),
        P("section", None, None),
        P("band", None),
        P("band"),
        P("band", None, None),
        P("band", None),
        P("band", None),
    )
    out_specs = (P("section", "band", None, None, None), P("band", None))
    local = make_local(mesh.shape["section"], mesh.shape["band"])
    return jax.shard_map(local, mesh=mesh, in_specs=in_specs, out_specs=out_specs, check_vma=False)
```

time: 181 us -> 121 us (0.67)
  other arithmetic: 37.3 us -> 0 us
  matrix products: 18.2 us -> 0 us
  Pallas kernels: 0 us -> 14.5 us
  blocking collectives: 79 us -> 66.7 us
  local copies, waits for them, and re-layouts: 9.71 us -> 1.37 us
    another operation x1 -> x0, other arithmetic: 36.7 us -> none
    dot_general x4 -> x0, matrix products: 18.2 us -> none  [the longest x1 6.85 us: local(): jnp.einsum('jqrm,mjrl->jql', fourier, lax.all_to_all(fields, 'band', spli...]
    psum x1 -> x0, blocking collectives: 17.2 us -> none  [local(): evolved = lax.psum(partial_obs, 'section')]
    pallas_call x0 -> x7, Pallas kernels: none -> 14.5 us  [the longest x1 3.65 us: forward_fields(): pl.pallas_call(functools.partial(forward_body, sections, bands), in_specs...]
    all_to_all x1 -> x3, blocking collectives: 61.9 us -> 66.7 us  [the longest x1 28.8 us: local(): lax.all_to_all(adjoint.reshape(bands, tile, levels), 'band', split_axis=0...]
    convert_element_type x2 -> x0, local copies, waits for them, and re-layouts: 4.59 us -> none  [the longest x1 2.47 us: observe(): return (departures, adjoint_fields.astype(jnp.bfloat16))]
    unnamed x17 -> x20, local copies, waits for them, and re-layouts: 3.9 us -> 1.37 us
  transfers between devices with their start and end apart: 1 -> 1, of which waited for: 1 -> 1; matrix products, arithmetic and copies ran while one was open for 22% -> 0% of each run, Pallas kernels for 0% -> 3%
where the time goes in v2:
time: 121 us; the launch traced here: 120 us
  blocking collectives  66.7 us (55%)
  starting transfers between devices  19 us (16%)
  waiting for transfers between devices  18.1 us (15%)
  Pallas kernels  14.5 us (12%)
  local copies, waits for them, and re-layouts  1.37 us (1%)
    all_to_all x1, blocking collectives, local(): lax.all_to_all(adjoint.reshape(bands, tile, levels), 'band', split_axis=0...  28.8 us
    all_to_all x1, blocking collectives, local(): lax.all_to_all(fields.reshape(sections, bands, tile, levels), 'section',...  19.5 us
    all_to_all x1, starting transfers between devices, local(): lax.all_to_all(field_sum.reshape(bands, tile, levels), 'band', split_axis...  19 us
    all_to_all x1, blocking collectives, local(): lax.all_to_all(pack(back.reshape(terms, levels), pieces, sections), 'sect...  18.4 us
    all_to_all x1, waiting for transfers between devices, local(): lax.all_to_all(field_sum.reshape(bands, tile, levels), 'band', split_axis...  18.1 us
    pallas_call x1, Pallas kernels, forward_fields(): pl.pallas_call(functools.partial(forward_body, sections, bands), in_specs...  3.65 us
    pallas_call x1, Pallas kernels, backward_gradient(): pl.pallas_call(backward_body, in_specs=[WHOLE] * 5, out_specs=[APART, WHO...  3.58 us
    pallas_call x1, Pallas kernels, observe(): pl.pallas_call(observe_body, in_specs=[SCALAR, SCALAR, WHOLE, WHOLE, APAR...  3.29 us
  transfers between devices with their start and end apart: 1, of which 1 were waited for; matrix products, arithmetic and copies ran while one was open for 0% of the time, Pallas kernels for 3%

profile of v2, /device:TPU:32, one launch (start us, length us, event | category | flops | bytes accessed | tf_op | source)
XLA Modules:
  0.0 120.4 jit_solution(15050412104570857666)
XLA Ops:
  0.6 3.7 %forward_fields.1 = bf16[4096,128]{1,0:T(8,128)(2,1)S(1)} custom-call(bf16[4,256,512]{2,1,0:T(8,128)(2,1)} %bitcast.12, bf16[4,512,512]{2,1,0:T(8,128)(2,1)} %legendre.3, f32[1,512]{1,0:T(1,128)} %spread.3, bf16[128,128]{1,0:T(8,128)(2,1)} %bitcast.17), custom_call_target="tpu_custom_call" | custom-call | tf_op jit(solution)/shard_map/forward_fields/pallas_call | solution.py:108
  4.3 0.0 copy-start
  4.3 19.5 %all_to_all.20 = bf16[4,128,8,128]{3,2,1,0:T(8,128)(2,1)S(1)} all-to-all(bf16[4,128,8,128]{3,2,1,0:T(8,128)(2,1)S(1)} %bitcast.11), channel_id=1, replica_groups=mesh['section'=4,'band'=128] {'section'}, dimensions={0} | all-to-all | bytes 2097152 | tf_op jit(solution)/shard_map/all_to_all | solution.py:326
  23.8 0.8 sum_sections.1
  24.6 19.0 %all-to-all-start.1 = ((bf16[128,8,128]{2,1,0:T(8,128)(2,1)}), bf16[128,8,128]{2,1,0:T(8,128)(2,1)S(1)}, u32[]{:S(2)}, u32[]{:S(2)}) async-start(bf16[128,8,128]{2,1,0:T(8,128)(2,1)} %bitcast.5), calls=%async_computation.1 | async-start | bytes 524288 | tf_op jit(solution)/shard_map/all_to_all | solution.py:331
  43.6 0.0 copy-done
  43.6 0.0 copy-start.5
  43.7 1.3 %regroup.1.grouped = bf16[4,512,512]{2,1,0:T(8,128)(2,1)S(1)} custom-call(bf16[4,512,512]{2,1,0:T(8,128)(2,1)S(1)} %copy-done), custom_call_target="tpu_custom_call" | custom-call | tf_op jit(solution)/shard_map/regroup/pallas_call | solution.py:233
  45.0 0.0 copy-start.1
  45.0 1.3 %copy-done.1 = bf16[4,512,512]{2,1,0:T(8,128)(2,1)} copy-done((bf16[4,512,512]{2,1,0:T(8,128)(2,1)}, bf16[4,512,512]{2,1,0:T(8,128)(2,1)S(1)}, u32[]{:S(2)}) %copy-start.1) | copy-done | bytes 2097176
  46.3 0.0 copy-start.6
  46.3 0.0 copy-start.7
  46.3 0.0 copy-start.9
  46.3 0.0 copy-done.5
  46.3 1.7 %make_basis.1.by_wave = bf16[1024,1024]{1,0:T(8,128)(2,1)S(1)} custom-call(s32[1]{0:T(128)} %bitcast.here, s32[4,1024]{1,0:T(4,128)S(1)} %copy-done.5), custom_call_target="tpu_custom_call" | custom-call | tf_op jit(solution)/shard_map/make_basis/pallas_call | solution.py:148
  48.1 18.1 %all-to-all-done.1 = bf16[128,8,128]{2,1,0:T(8,128)(2,1)S(1)} async-done(((bf16[128,8,128]{2,1,0:T(8,128)(2,1)}), bf16[128,8,128]{2,1,0:T(8,128)(2,1)S(1)}, u32[]{:S(2)}, u32[]{:S(2)}) %all-to-all-start.1) | async-done | bytes 262176 | tf_op jit(solution)/shard_map/all_to_all | solution.py:331
  66.1 0.0 copy-done.6
  66.1 0.0 copy-done.7
  66.1 0.0 copy-done.9
  66.1 3.3 %observe.1 = (bf16[1024,128]{1,0:T(8,128)(2,1)S(1)}, bf16[24,128]{1,0:T(8,128)(2,1)S(1)}) custom-call(s32[1]{0:T(128)} %bitcast.here, s32[4]{0:T(128)S(1)} %copy-done.9, bf16[1024,1024]{1,0:T(8,128)(2,1)S(1)} %make_basis.1.by_wave, bf16[1024,128]{1,0:T(8,128)(2,1)S(1)} %bitcast.14, bf16[4,1024,128]{2,1,0:T(8,128)(2,1)} %kernels.1, f32[4,1024]{1,0:T(4,128)S(1)} %copy-done.6, ...), custom_call_target="tpu_custom_call" | custom-call | tf_op jit(solution)/shard_map/observe/pallas_call | solution.py:193
  69.4 0.0 copy-start.2
  69.4 0.0 copy-start.3
  69.5 0.0 copy-start.4
  69.5 0.0 copy-start.8
  69.5 28.8 %all_to_all.21 = bf16[128,8,128]{2,1,0:T(8,128)(2,1)S(1)} all-to-all(bf16[128,8,128]{2,1,0:T(8,128)(2,1)S(1)} %bitcast.16), channel_id=1, replica_groups=mesh['section'=4,'band'=128] {'band'}, dimensions={0} | all-to-all | bytes 524288 | tf_op jit(solution)/shard_map/all_to_all | solution.py:342
  98.3 0.1 pack.1
  98.4 18.4 %all_to_all.22.packets = bf16[4,1048,128]{2,1,0:T(8,128)(2,1)S(1)} all-to-all(bf16[4,1048,128]{2,1,0:T(8,128)(2,1)S(1)} %pack.1), channel_id=1, replica_groups=mesh['section'=4,'band'=128] {'section'}, dimensions={0} | all-to-all | bytes 2146304 | tf_op jit(solution)/shard_map/all_to_all | solution.py:345
  116.8 0.0 copy-done.2
  116.8 0.0 copy-done.3
  116.8 0.0 copy-done.4
  116.8 0.0 copy-done.8
  116.9 3.6 %backward_gradient.1 = (bf16[4,256,512]{2,1,0:T(8,128)(2,1)}, f32[4,1024]{1,0:T(4,128)}) custom-call(bf16[4,1048,128]{2,1,0:T(8,128)(2,1)S(1)} %all_to_all.22.packets, bf16[4,512,512]{2,1,0:T(8,128)(2,1)S(1)} %copy-done.2, bf16[4,256,512]{2,1,0:T(8,128)(2,1)S(1)} %bitcast.13, f32[1,512]{1,0:T(1,128)S(1)} %copy-done.8, bf16[128,128]{1,0:T(8,128)(2,1)S(1)} %bitcast.18), custom_call_target="tpu_custom_call" | custom-call | tf_op jit(solution)/shard_map/backward_gradient/pallas_call | solution.py:294
Async XLA Ops:
  4.3 39.4 %copy-start = (bf16[4,512,512]{2,1,0:T(8,128)(2,1)S(1)}, bf16[4,512,512]{2,1,0:T(8,128)(2,1)}, u32[]{:S(2)}) copy-start(bf16[4,512,512]{2,1,0:T(8,128)(2,1)} %legendre.3) | copy-start | bytes 6291460
  24.6 41.5 %all-to-all-start.1 = ((bf16[128,8,128]{2,1,0:T(8,128)(2,1)}), bf16[128,8,128]{2,1,0:T(8,128)(2,1)S(1)}, u32[]{:S(2)}, u32[]{:S(2)}) async-start(bf16[128,8,128]{2,1,0:T(8,128)(2,1)} %bitcast.5), calls=%async_computation.1 | async-start | bytes 524288 | tf_op jit(solution)/shard_map/all_to_all | solution.py:331
  43.6 2.7 %copy-start.5 = (s32[4,1024]{1,0:T(4,128)S(1)}, s32[4,1024]{1,0:T(4,128)}, u32[]{:S(2)}) copy-start(s32[4,1024]{1,0:T(4,128)} %obs_lon.1) | copy-start | bytes 49156
  45.0 1.3 %copy-start.1 = (bf16[4,512,512]{2,1,0:T(8,128)(2,1)}, bf16[4,512,512]{2,1,0:T(8,128)(2,1)S(1)}, u32[]{:S(2)}) copy-start(bf16[4,512,512]{2,1,0:T(8,128)(2,1)S(1)} %regroup.1.grouped) | copy-start | bytes 6291460
  46.3 19.8 %copy-start.6 = (f32[4,1024]{1,0:T(4,128)S(1)}, f32[4,1024]{1,0:T(4,128)}, u32[]{:S(2)}) copy-start(f32[4,1024]{1,0:T(4,128)} %value.1) | copy-start | bytes 49156
  46.3 19.8 %copy-start.7 = (f32[4,1024]{1,0:T(4,128)S(1)}, f32[4,1024]{1,0:T(4,128)}, u32[]{:S(2)}) copy-start(f32[4,1024]{1,0:T(4,128)} %weight.1) | copy-start | bytes 49156
  46.3 19.8 %copy-start.9 = (s32[4]{0:T(128)S(1)}, s32[4]{0:T(128)}, u32[]{:S(2)}) copy-start(s32[4]{0:T(128)} %count.1) | copy-start | bytes 52
  69.4 47.4 %copy-start.2 = (bf16[4,512,512]{2,1,0:T(8,128)(2,1)S(1)}, bf16[4,512,512]{2,1,0:T(8,128)(2,1)}, u32[]{:S(2)}) copy-start(bf16[4,512,512]{2,1,0:T(8,128)(2,1)} %copy-done.1) | copy-start | bytes 6291460
  69.4 47.4 %copy-start.3 = (bf16[1,4,2,128,512]{4,3,2,1,0:T(8,128)(2,1)S(1)}, bf16[1,4,2,128,512]{4,3,2,1,0:T(8,128)(2,1)}, u32[]{:S(2)}) copy-start(bf16[1,4,2,128,512]{4,3,2,1,0:T(8,128)(2,1)} %param.9) | copy-start | bytes 3145732
  69.5 47.4 %copy-start.4 = (bf16[1,128,128]{2,1,0:T(8,128)(2,1)S(1)}, bf16[1,128,128]{2,1,0:T(8,128)(2,1)}, u32[]{:S(2)}) copy-start(bf16[1,128,128]{2,1,0:T(8,128)(2,1)} %param.12) | copy-start | bytes 98308
  69.5 47.4 %copy-start.8 = (f32[1,512]{1,0:T(1,128)S(1)}, f32[1,512]{1,0:T(1,128)}, u32[]{:S(2)}) copy-start(f32[1,512]{1,0:T(1,128)} %spread.3) | copy-start | bytes 6148

commit v3 on v2

--- a/solution.py
+++ b/solution.py
@@ -74,7 +74,9 @@
     order = [(spread, spreads), (mixing, mixings)]
     for m in range(waves_here):
         order += [(control.at[m], coeffs.at[m]), (legendre.at[m], basis.at[m])]
-    copies = pull(order, sems)
+    copies = [pltpu.make_async_copy(a, b, sems.at[i]) for i, (a, b) in enumerate(order)]
+    for copy in copies[:6]:
+        copy.start()
     copies[0].wait()
     copies[1].wait()
     diagonal[...] = jnp.zeros_like(diagonal)
@@ -84,6 +86,8 @@
     for m in range(waves_here):
         copies[2 + 2 * m].wait()
         copies[3 + 2 * m].wait()
+        for copy in copies[6 + 2 * m : 8 + 2 * m]:
+            copy.start()
         scaled = (coeffs[m].astype(F32) * spreads[...]).astype(BF16)
         rows = lax.dot_general(
             basis[m], scaled, (((0,), (1,)), ((), ())), preferred_element_type=F32
@@ -129,9 +133,11 @@
     return jnp.cos(angle), jnp.sin(angle)
 
 
-def basis_body(here, obs_lon, by_wave):
-    terms, _ = by_wave.shape
-    lon = obs_lon[pl.ds(here[0], 1), :]
+def basis_body(here, count, obs_lon, value, weight, kernels, by_wave, turned, lines, kern, sems):
+    copy = pull([(kernels.at[here[0]], kern)], sems)[0]
+    terms, slots = by_wave.shape
+    line = pl.ds(here[0], 1)
+    lon = obs_lon[line, :]
     fine = lax.broadcasted_iota(jnp.int32, (FINE, 1), 0)
     coarse = lax.broadcasted_iota(jnp.int32, (terms // FINE, 1), 0)
     fine_cos, fine_sin = turn(lax.shift_right_logical(fine, 1) * lon + (fine & 1) * (NLON // 4))
@@ -142,67 +148,63 @@
         if a == 0:
             block = jnp.where(fine < 2, fine_cos, block)
         by_wave[pl.ds(a * FINE, FINE), :] = block.astype(BF16)
-
-
-def make_basis(here, obs_lon, terms):
+    slot = lax.broadcasted_iota(jnp.int32, (1, slots), 1)
+    lines[pl.ds(0, 1), :] = value[line, :]
+    lines[pl.ds(1, 1), :] = weight[line, :]
+    lines[pl.ds(2, 1), :] = jnp.where(slot < count[here[0]], 1.0, 0.0)
+    levels = kern.shape[1]
+    eye = lax.broadcasted_iota(jnp.int32, (levels, levels), 0) == lax.broadcasted_iota(
+        jnp.int32, (levels, levels), 1
+    )
+    copy.wait()
+    turned[...] = dot_minor(jnp.where(eye, 1.0, 0.0).astype(BF16), kern[...]).astype(BF16)
+
+
+def make_basis(here, count, obs_lon, value, weight, kernels, terms):
+    _, slots, levels = kernels.shape
     return pl.pallas_call(
         basis_body,
-        in_specs=[SCALAR, WHOLE],
-        out_specs=WHOLE,
-        out_shape=made((terms, obs_lon.shape[1]), BF16),
+        in_specs=[SCALAR, SCALAR, WHOLE, WHOLE, WHOLE, APART],
+        out_specs=[WHOLE] * 3,
+        out_shape=[
+            made((terms, slots), BF16),
+            made((levels, slots), BF16),
+            made((8, slots), F32),
+        ],
+        scratch_shapes=[pltpu.VMEM((slots, levels), BF16), pltpu.SemaphoreType.DMA((1,))],
         name="make_basis",
         compiler_params=LIMIT,
-    )(here, obs_lon)
-
-
-def observe_body(
-    here, count, by_wave, fields, kernels, value, weight, adjoint, pieces, kern, departures, sems
-):
-    copy = pull([(kernels.at[here[0]], kern)], sems)[0]
-    columns = lax.dot_general(
-        by_wave[...], fields[...], (((0,), (0,)), ((), ())), preferred_element_type=F32
-    )
-    slots, lanes = kern.shape
-    half = lanes // 2
-    line = pl.ds(here[0], 1)
-    rows = [jnp.broadcast_to(part[line, :], (half, slots)) for part in (value, weight)]
-    known = jnp.concatenate(rows, axis=0).T
-    copy.wait()
+    )(here, count, obs_lon, value, weight, far(kernels))
+
+
+def observe_body(by_wave, fields, kern, lines, adjoint, pieces, departures):
+    columns = dot(fields[...].T, by_wave[...])
     wide = kern[...].astype(F32)
-    evolved = jnp.sum(wide * columns, axis=1, keepdims=True)
-    slot = lax.broadcasted_iota(jnp.int32, evolved.shape, 0)
-    departed = jnp.where(slot < count[here[0]], evolved - known[:, :1], 0.0)
-    scaled = (known[:, half : half + 1] * departed * wide).astype(BF16)
-    adjoint[...] = dot(by_wave[...], scaled).astype(BF16)
-    diagonal = lax.broadcasted_iota(jnp.int32, (lanes, lanes), 0) == lax.broadcasted_iota(
-        jnp.int32, (lanes, lanes), 1
-    )
-    for i in range(slots // lanes):
-        spot = jnp.where(diagonal, departed[i * lanes : (i + 1) * lanes], 0.0)
-        departures[pl.ds(i, 1), :] = jnp.sum(spot, axis=0, keepdims=True)
+    evolved = jnp.sum(wide * columns, axis=0, keepdims=True)
+    departed = jnp.where(lines[pl.ds(2, 1), :] > 0.5, evolved - lines[pl.ds(0, 1), :], 0.0)
+    scaled = (lines[pl.ds(1, 1), :] * departed * wide).astype(BF16)
+    adjoint[...] = dot_minor(scaled, by_wave[...]).T.astype(BF16)
+    size, lanes = departures.shape
+    for i in range(size):
+        departures[pl.ds(i, 1), :] = departed[:, i * lanes : (i + 1) * lanes]
     rest = departures[...]
-    size = rest.shape[0]
     for i in range(3):
         piece = rest.astype(BF16)
         pieces[pl.ds(i * size, size), :] = piece
         rest = rest - piece.astype(F32)
 
 
-def observe(here, count, by_wave, fields, kernels, value, weight):
-    _, slots, levels = kernels.shape
+def observe(by_wave, fields, kern, lines):
+    levels, slots = kern.shape
     return pl.pallas_call(
         observe_body,
-        in_specs=[SCALAR, SCALAR, WHOLE, WHOLE, APART, WHOLE, WHOLE],
+        in_specs=[WHOLE] * 4,
         out_specs=[WHOLE, WHOLE],
         out_shape=[made(fields.shape, BF16), made((3 * slots // levels, levels), BF16)],
-        scratch_shapes=[
-            pltpu.VMEM((slots, levels), BF16),
-            pltpu.VMEM((slots // levels, levels), F32),
-            pltpu.SemaphoreType.DMA((1,)),
-        ],
+        scratch_shapes=[pltpu.VMEM((slots // levels, levels), F32)],
         name="observe",
         compiler_params=LIMIT,
-    )(here, count, near(by_wave), near(fields), far(kernels), near(value), near(weight))
+    )(near(by_wave), near(fields), near(kern), near(lines))
 
 
 def sum_body(parts, out):
@@ -240,48 +242,57 @@
     )(legendre)
 
 
-def pack_body(body, pieces, out):
+def pack_body(tile, body, pieces, out, held):
+    held[...] = body[...].astype(F32)
     rows = body.shape[0]
+    run = rows // tile
+    for i in range(tile):
+        block = held[pl.ds(i, run, stride=tile), :].astype(BF16)
+        for section in range(out.shape[0]):
+            out[section, pl.ds(i * run, run), :] = block
     for section in range(out.shape[0]):
-        out[section, pl.ds(0, rows), :] = body[...]
         out[section, pl.ds(rows, pieces.shape[0]), :] = pieces[...]
 
 
-def pack(body, pieces, sections):
+def pack(body, pieces, sections, tile):
     rows = body.shape[0] + pieces.shape[0]
     return pl.pallas_call(
-        pack_body,
+        functools.partial(pack_body, tile),
         in_specs=[WHOLE, WHOLE],
         out_specs=WHOLE,
         out_shape=made((sections, rows, body.shape[1]), BF16),
+        scratch_shapes=[pltpu.VMEM(body.shape, F32)],
         name="pack",
         compiler_params=LIMIT,
     )(near(body), near(pieces))
 
 
-def backward_body(packets, grouped, control, spread, mixing, out, departures, held, ready, sems):
+def backward_body(
+    packets, grouped, control, spread, mixing, out, all_departures, ready, departures, sems
+):
     sections, _, levels = packets.shape
     waves_here = grouped.shape[0]
-    latitudes = grouped.shape[2]
-    tile = 2 * waves_here
-    size = latitudes // sections * tile
+    run = grouped.shape[2] // sections
+    size = run * 2 * waves_here
     mixing_t = mixing[...].astype(F32).T.astype(BF16)
     lines = departures.shape[1] // levels
     for t in range(sections):
-        held[pl.ds(t * size, size), :] = packets[t, pl.ds(0, size), :].astype(F32)
         parts = [packets[t, pl.ds(size + i * lines, lines), :].astype(F32) for i in range(3)]
         whole = (parts[2] + parts[1]) + parts[0]
         for i in range(lines):
             departures[pl.ds(t, 1), pl.ds(i * levels, levels)] = whole[i : i + 1]
-    leaving = []
+    leaving = pull([(departures, all_departures)], sems)
     for m in range(waves_here):
-        rows = [held[pl.ds(2 * m + r, latitudes, stride=tile), :].astype(BF16) for r in range(2)]
+        rows = [
+            jnp.concatenate([packets[t, pl.ds((2 * m + r) * run, run), :] for t in range(sections)])
+            for r in range(2)
+        ]
         terms = dot(grouped[m], jnp.concatenate(rows, axis=1)).astype(BF16)
         for r in range(2):
             part = pl.ds(r * levels, levels)
             total = dot_minor(mixing_t, terms[:, r * levels : (r + 1) * levels])
             ready[m, part, :] = (control[m, part, :].astype(F32) + spread[...] * total).astype(BF16)
-        copy = pltpu.make_async_copy(ready.at[m], out.at[m], sems.at[m])
+        copy = pltpu.make_async_copy(ready.at[m], out.at[m], sems.at[m + 1])
         copy.start()
         leaving.append(copy)
     for copy in leaving:
@@ -289,20 +300,20 @@
 
 
 def backward_gradient(packets, grouped, control, spread, mixing, slots):
-    sections, _, levels = packets.shape
-    waves_here, _, latitudes = grouped.shape
+    sections = packets.shape[0]
+    waves_here = grouped.shape[0]
     return pl.pallas_call(
         backward_body,
         in_specs=[WHOLE] * 5,
-        out_specs=[APART, WHOLE],
+        out_specs=[APART, APART],
         out_shape=[
             jax.ShapeDtypeStruct(control.shape, BF16),
             jax.ShapeDtypeStruct((sections, slots), F32),
         ],
         scratch_shapes=[
-            pltpu.VMEM((latitudes * 2 * waves_here, levels), F32),
             pltpu.VMEM(control.shape, BF16),
-            pltpu.SemaphoreType.DMA((waves_here,)),
+            pltpu.VMEM((sections, slots), F32),
+            pltpu.SemaphoreType.DMA((1 + waves_here,)),
         ],
         name="backward_gradient",
         compiler_params=LIMIT,
@@ -332,18 +343,18 @@
             field_sum.reshape(bands, tile, levels), "band", split_axis=0, concat_axis=0, tiled=True
         )
 
-        by_wave = make_basis(here[None], obs_lon, terms)
+        tables = make_basis(
+            here[None], obs_count, obs_lon, obs_value, obs_weight, kernels, terms
+        )
         grouped = regroup(legendre, sections, bands)
-        row_fields, by_wave, grouped = lax.optimization_barrier((row_fields, by_wave, grouped))
-        adjoint, pieces = observe(
-            here[None], obs_count, by_wave, row_fields.reshape(terms, levels),
-            kernels, obs_value, obs_weight,
-        )
+        row_fields, tables, grouped = lax.optimization_barrier((row_fields, tables, grouped))
+        by_wave, kern, lines = tables
+        adjoint, pieces = observe(by_wave, row_fields.reshape(terms, levels), kern, lines)
         back = lax.all_to_all(
             adjoint.reshape(bands, tile, levels), "band", split_axis=0, concat_axis=0, tiled=True
         )
         packets = lax.all_to_all(
-            pack(back.reshape(terms, levels), pieces, sections),
+            pack(back.reshape(terms, levels), pieces, sections, tile),
             "section", split_axis=0, concat_axis=0, tiled=True,
         )
         gradient, all_departures = backward_gradient(

time: 121 us -> 118 us (0.975)
  Pallas kernels: 14.5 us -> 12.7 us
    pallas_call x4, Pallas kernels: 8.76 us -> 6.91 us  [the longest x1 2.9 us: backward_gradient(): pl.pallas_call(backward_body, in_specs=[WHOLE] * 5, out_specs=[APART, APA...]
where the time goes in v3:
time: 118 us
  blocking collectives  66.7 us (57%)
  starting transfers between devices  19 us (16%)
  waiting for transfers between devices  17.2 us (15%)
  Pallas kernels  12.7 us (11%)
  local copies, waits for them, and re-layouts  1.39 us (1%)
    all_to_all x1, blocking collectives, local(): lax.all_to_all(adjoint.reshape(bands, tile, levels), 'band', split_axis=0...  28.8 us
    all_to_all x1, blocking collectives, local(): lax.all_to_all(fields.reshape(sections, bands, tile, levels), 'section',...  19.5 us
    all_to_all x1, starting transfers between devices, local(): lax.all_to_all(field_sum.reshape(bands, tile, levels), 'band', split_axis...  19 us
    all_to_all x1, blocking collectives, local(): lax.all_to_all(pack(back.reshape(terms, levels), pieces, sections, tile),...  18.4 us
    all_to_all x1, waiting for transfers between devices, local(): lax.all_to_all(field_sum.reshape(bands, tile, levels), 'band', split_axis...  17.2 us
    pallas_call x1, Pallas kernels, forward_fields(): pl.pallas_call(functools.partial(forward_body, sections, bands), in_specs...  3.67 us
    pallas_call x1, Pallas kernels, backward_gradient(): pl.pallas_call(backward_body, in_specs=[WHOLE] * 5, out_specs=[APART, APA...  2.9 us
    pallas_call x1, Pallas kernels, make_basis(): pl.pallas_call(basis_body, in_specs=[SCALAR, SCALAR, WHOLE, WHOLE, WHOLE,...  2.56 us
  transfers between devices with their start and end apart: 1, of which 1 were waited for; matrix products, arithmetic and copies ran while one was open for 0% of the time, Pallas kernels for 3%

profile of v3, /device:TPU:32, one launch (start us, length us, event | category | flops | bytes accessed | tf_op | source)
XLA Modules:
  0.0 117.8 jit_solution(5328210018672944969)
XLA Ops:
  0.6 3.7 %forward_fields.1 = bf16[4096,128]{1,0:T(8,128)(2,1)S(1)} custom-call(bf16[4,256,512]{2,1,0:T(8,128)(2,1)} %bitcast.12, bf16[4,512,512]{2,1,0:T(8,128)(2,1)} %legendre.3, f32[1,512]{1,0:T(1,128)} %spread.3, bf16[128,128]{1,0:T(8,128)(2,1)} %bitcast.17), custom_call_target="tpu_custom_call" | custom-call | tf_op jit(solution)/shard_map/forward_fields/pallas_call | solution.py:112
  4.3 0.0 copy-start
  4.3 19.5 %all_to_all.20 = bf16[4,128,8,128]{3,2,1,0:T(8,128)(2,1)S(1)} all-to-all(bf16[4,128,8,128]{3,2,1,0:T(8,128)(2,1)S(1)} %bitcast.11), channel_id=1, replica_groups=mesh['section'=4,'band'=128] {'section'}, dimensions={0} | all-to-all | bytes 2097152 | tf_op jit(solution)/shard_map/all_to_all | solution.py:337
  23.8 0.8 sum_sections.1
  24.6 19.0 %all-to-all-start.1 = ((bf16[128,8,128]{2,1,0:T(8,128)(2,1)}), bf16[128,8,128]{2,1,0:T(8,128)(2,1)S(1)}, u32[]{:S(2)}, u32[]{:S(2)}) async-start(bf16[128,8,128]{2,1,0:T(8,128)(2,1)} %bitcast.4), calls=%async_computation.1 | async-start | bytes 524288 | tf_op jit(solution)/shard_map/all_to_all | solution.py:342
  43.7 0.0 copy-done
  43.7 0.0 copy-start.5
  43.7 0.0 copy-start.6
  43.7 0.0 copy-start.7
  43.7 0.0 copy-start.9
  43.7 1.3 %regroup.1.grouped = bf16[4,512,512]{2,1,0:T(8,128)(2,1)S(1)} custom-call(bf16[4,512,512]{2,1,0:T(8,128)(2,1)S(1)} %copy-done), custom_call_target="tpu_custom_call" | custom-call | tf_op jit(solution)/shard_map/regroup/pallas_call | solution.py:235
  45.0 0.0 copy-start.1
  45.0 1.3 %copy-done.1 = bf16[4,512,512]{2,1,0:T(8,128)(2,1)} copy-done((bf16[4,512,512]{2,1,0:T(8,128)(2,1)}, bf16[4,512,512]{2,1,0:T(8,128)(2,1)S(1)}, u32[]{:S(2)}) %copy-start.1) | copy-done | bytes 2097176
  46.4 0.0 copy-done.5
  46.4 0.0 copy-done.6
  46.4 0.0 copy-done.7
  46.4 0.0 copy-done.9
  46.4 2.6 %make_basis.1 = (bf16[1024,1024]{1,0:T(8,128)(2,1)S(1)}, bf16[128,1024]{1,0:T(8,128)(2,1)S(1)}, f32[8,1024]{1,0:T(8,128)S(1)}) custom-call(s32[1]{0:T(128)} %bitcast.5.here, s32[4]{0:T(128)S(1)} %copy-done.9, s32[4,1024]{1,0:T(4,128)S(1)} %copy-done.5, f32[4,1024]{1,0:T(4,128)S(1)} %copy-done.6, f32[4,1024]{1,0:T(4,128)S(1)} %copy-done.7, ...), custom_call_target="tpu_custom_call" | custom-call | tf_op jit(solution)/shard_map/make_basis/pallas_call | solution.py:165
  48.9 17.2 %all-to-all-done.1 = bf16[128,8,128]{2,1,0:T(8,128)(2,1)S(1)} async-done(((bf16[128,8,128]{2,1,0:T(8,128)(2,1)}), bf16[128,8,128]{2,1,0:T(8,128)(2,1)S(1)}, u32[]{:S(2)}, u32[]{:S(2)}) %all-to-all-start.1) | async-done | bytes 262176 | tf_op jit(solution)/shard_map/all_to_all | solution.py:342
  66.2 1.3 %observe.1 = (bf16[1024,128]{1,0:T(8,128)(2,1)S(1)}, bf16[24,128]{1,0:T(8,128)(2,1)S(1)}) custom-call(bf16[1024,1024]{1,0:T(8,128)(2,1)S(1)} %get-tuple-element.17.by_wave, bf16[1024,128]{1,0:T(8,128)(2,1)S(1)} %bitcast.15, bf16[128,1024]{1,0:T(8,128)(2,1)S(1)} %get-tuple-element.19.kern, f32[8,1024]{1,0:T(8,128)S(1)} %get-tuple-element.20.lines), custom_call_target="tpu_custom_call" | custom-call | tf_op jit(solution)/shard_map/observe/pallas_call | solution.py:199
  67.5 0.0 copy-start.2
  67.5 0.0 copy-start.3
  67.5 0.0 copy-start.4
  67.5 0.0 copy-start.8
  67.5 28.8 %all_to_all.21 = bf16[128,8,128]{2,1,0:T(8,128)(2,1)S(1)} all-to-all(bf16[128,8,128]{2,1,0:T(8,128)(2,1)S(1)} %bitcast.16), channel_id=1, replica_groups=mesh['section'=4,'band'=128] {'band'}, dimensions={0} | all-to-all | bytes 524288 | tf_op jit(solution)/shard_map/all_to_all | solution.py:353
  96.3 0.1 pack.1
  96.5 18.4 %all_to_all.22.packets = bf16[4,1048,128]{2,1,0:T(8,128)(2,1)S(1)} all-to-all(bf16[4,1048,128]{2,1,0:T(8,128)(2,1)S(1)} %pack.1), channel_id=1, replica_groups=mesh['section'=4,'band'=128] {'section'}, dimensions={0} | all-to-all | bytes 2146304 | tf_op jit(solution)/shard_map/all_to_all | solution.py:356
  114.9 0.0 copy-done.2
  114.9 0.0 copy-done.3
  114.9 0.0 copy-done.4
  114.9 0.0 copy-done.8
  114.9 2.9 %backward_gradient.1 = (bf16[4,256,512]{2,1,0:T(8,128)(2,1)}, f32[4,1024]{1,0:T(4,128)}) custom-call(bf16[4,1048,128]{2,1,0:T(8,128)(2,1)S(1)} %all_to_all.22.packets, bf16[4,512,512]{2,1,0:T(8,128)(2,1)S(1)} %copy-done.2, bf16[4,256,512]{2,1,0:T(8,128)(2,1)S(1)} %bitcast.13, f32[1,512]{1,0:T(1,128)S(1)} %copy-done.8, bf16[128,128]{1,0:T(8,128)(2,1)S(1)} %bitcast.18), custom_call_target="tpu_custom_call" | custom-call | tf_op jit(solution)/shard_map/backward_gradient/pallas_call | solution.py:305
Async XLA Ops:
  4.3 39.4 %copy-start = (bf16[4,512,512]{2,1,0:T(8,128)(2,1)S(1)}, bf16[4,512,512]{2,1,0:T(8,128)(2,1)}, u32[]{:S(2)}) copy-start(bf16[4,512,512]{2,1,0:T(8,128)(2,1)} %legendre.3) | copy-start | bytes 6291460
  24.6 41.5 %all-to-all-start.1 = ((bf16[128,8,128]{2,1,0:T(8,128)(2,1)}), bf16[128,8,128]{2,1,0:T(8,128)(2,1)S(1)}, u32[]{:S(2)}, u32[]{:S(2)}) async-start(bf16[128,8,128]{2,1,0:T(8,128)(2,1)} %bitcast.4), calls=%async_computation.1 | async-start | bytes 524288 | tf_op jit(solution)/shard_map/all_to_all | solution.py:342
  43.7 2.7 %copy-start.5 = (s32[4,1024]{1,0:T(4,128)S(1)}, s32[4,1024]{1,0:T(4,128)}, u32[]{:S(2)}) copy-start(s32[4,1024]{1,0:T(4,128)} %obs_lon.1) | copy-start | bytes 49156
  43.7 2.7 %copy-start.6 = (f32[4,1024]{1,0:T(4,128)S(1)}, f32[4,1024]{1,0:T(4,128)}, u32[]{:S(2)}) copy-start(f32[4,1024]{1,0:T(4,128)} %value.1) | copy-start | bytes 49156
  43.7 2.7 %copy-start.7 = (f32[4,1024]{1,0:T(4,128)S(1)}, f32[4,1024]{1,0:T(4,128)}, u32[]{:S(2)}) copy-start(f32[4,1024]{1,0:T(4,128)} %weight.1) | copy-start | bytes 49156
  43.7 2.7 %copy-start.9 = (s32[4]{0:T(128)S(1)}, s32[4]{0:T(128)}, u32[]{:S(2)}) copy-start(s32[4]{0:T(128)} %count.1) | copy-start | bytes 52
  45.0 1.3 %copy-start.1 = (bf16[4,512,512]{2,1,0:T(8,128)(2,1)}, bf16[4,512,512]{2,1,0:T(8,128)(2,1)S(1)}, u32[]{:S(2)}) copy-start(bf16[4,512,512]{2,1,0:T(8,128)(2,1)S(1)} %regroup.1.grouped) | copy-start | bytes 6291460
  67.5 47.4 %copy-start.2 = (bf16[4,512,512]{2,1,0:T(8,128)(2,1)S(1)}, bf16[4,512,512]{2,1,0:T(8,128)(2,1)}, u32[]{:S(2)}) copy-start(bf16[4,512,512]{2,1,0:T(8,128)(2,1)} %copy-done.1) | copy-start | bytes 6291460
  67.5 47.4 %copy-start.3 = (bf16[1,4,2,128,512]{4,3,2,1,0:T(8,128)(2,1)S(1)}, bf16[1,4,2,128,512]{4,3,2,1,0:T(8,128)(2,1)}, u32[]{:S(2)}) copy-start(bf16[1,4,2,128,512]{4,3,2,1,0:T(8,128)(2,1)} %param.9) | copy-start | bytes 3145732
  67.5 47.4 %copy-start.4 = (bf16[1,128,128]{2,1,0:T(8,128)(2,1)S(1)}, bf16[1,128,128]{2,1,0:T(8,128)(2,1)}, u32[]{:S(2)}) copy-start(bf16[1,128,128]{2,1,0:T(8,128)(2,1)} %param.12) | copy-start | bytes 98308
  67.5 47.4 %copy-start.8 = (f32[1,512]{1,0:T(1,128)S(1)}, f32[1,512]{1,0:T(1,128)}, u32[]{:S(2)}) copy-start(f32[1,512]{1,0:T(1,128)} %spread.3) | copy-start | bytes 6148

commit v4 on v3

--- a/solution.py
+++ b/solution.py
@@ -194,14 +194,14 @@
         rest = rest - piece.astype(F32)
 
 
-def observe(by_wave, fields, kern, lines):
-    levels, slots = kern.shape
+def observe(by_wave, fields, kern, lines, lanes):
+    _, slots = kern.shape
     return pl.pallas_call(
         observe_body,
         in_specs=[WHOLE] * 4,
         out_specs=[WHOLE, WHOLE],
-        out_shape=[made(fields.shape, BF16), made((3 * slots // levels, levels), BF16)],
-        scratch_shapes=[pltpu.VMEM((slots // levels, levels), F32)],
+        out_shape=[made(fields.shape, BF16), made((3 * slots // lanes, lanes), BF16)],
+        scratch_shapes=[pltpu.VMEM((slots // lanes, lanes), F32)],
         name="observe",
         compiler_params=LIMIT,
     )(near(by_wave), near(fields), near(kern), near(lines))
@@ -228,15 +228,16 @@
 def regroup_body(sections, bands, legendre, out):
     group = grouping(sections, bands)
     for m in range(legendre.shape[0]):
-        out[m] = dot_minor(legendre[m], group).astype(BF16)
+        out[m] = dot_minor(group, legendre[m]).astype(BF16)
 
 
 def regroup(legendre, sections, bands):
+    waves_here, numbers, latitudes = legendre.shape
     return pl.pallas_call(
         functools.partial(regroup_body, sections, bands),
         in_specs=[WHOLE],
         out_specs=WHOLE,
-        out_shape=jax.ShapeDtypeStruct(legendre.shape, BF16),
+        out_shape=jax.ShapeDtypeStruct((waves_here, latitudes, numbers), BF16),
         name="regroup",
         compiler_params=LIMIT,
     )(legendre)
@@ -244,23 +245,25 @@
 
 def pack_body(tile, body, pieces, out, held):
     held[...] = body[...].astype(F32)
-    rows = body.shape[0]
+    rows, levels = body.shape
     run = rows // tile
+    size = tile * levels
     for i in range(tile):
-        block = held[pl.ds(i, run, stride=tile), :].astype(BF16)
+        block = held[pl.ds(i, run, stride=tile), :].T.astype(BF16)
         for section in range(out.shape[0]):
-            out[section, pl.ds(i * run, run), :] = block
+            out[section, pl.ds(i * levels, levels), :] = block
     for section in range(out.shape[0]):
-        out[section, pl.ds(rows, pieces.shape[0]), :] = pieces[...]
+        out[section, pl.ds(size, pieces.shape[0]), :] = pieces[...]
 
 
 def pack(body, pieces, sections, tile):
-    rows = body.shape[0] + pieces.shape[0]
+    levels = body.shape[1]
+    rows = tile * levels + pieces.shape[0]
     return pl.pallas_call(
         functools.partial(pack_body, tile),
         in_specs=[WHOLE, WHOLE],
         out_specs=WHOLE,
-        out_shape=made((sections, rows, body.shape[1]), BF16),
+        out_shape=made((sections, rows, body.shape[0] // tile), BF16),
         scratch_shapes=[pltpu.VMEM(body.shape, F32)],
         name="pack",
         compiler_params=LIMIT,
@@ -268,30 +271,31 @@
 
 
 def backward_body(
-    packets, grouped, control, spread, mixing, out, all_departures, ready, departures, sems
+    packets, grouped, control, spread, mixing, out, all_departures,
+    ready, departures, diagonal, sems,
 ):
-    sections, _, levels = packets.shape
+    sections, _, lanes = packets.shape
     waves_here = grouped.shape[0]
-    run = grouped.shape[2] // sections
-    size = run * 2 * waves_here
-    mixing_t = mixing[...].astype(F32).T.astype(BF16)
-    lines = departures.shape[1] // levels
+    levels = mixing.shape[0]
+    size = levels * 2 * waves_here
+    lines = departures.shape[1] // lanes
     for t in range(sections):
         parts = [packets[t, pl.ds(size + i * lines, lines), :].astype(F32) for i in range(3)]
         whole = (parts[2] + parts[1]) + parts[0]
         for i in range(lines):
-            departures[pl.ds(t, 1), pl.ds(i * levels, levels)] = whole[i : i + 1]
+            departures[pl.ds(t, 1), pl.ds(i * lanes, lanes)] = whole[i : i + 1]
     leaving = pull([(departures, all_departures)], sems)
+    mixing_t = mixing[...].astype(F32).T.astype(BF16)
+    diagonal[...] = jnp.zeros_like(diagonal)
+    for r in range(2):
+        part = pl.ds(r * levels, levels)
+        diagonal[part, part] = mixing_t
     for m in range(waves_here):
-        rows = [
-            jnp.concatenate([packets[t, pl.ds((2 * m + r) * run, run), :] for t in range(sections)])
-            for r in range(2)
-        ]
-        terms = dot(grouped[m], jnp.concatenate(rows, axis=1)).astype(BF16)
-        for r in range(2):
-            part = pl.ds(r * levels, levels)
-            total = dot_minor(mixing_t, terms[:, r * levels : (r + 1) * levels])
-            ready[m, part, :] = (control[m, part, :].astype(F32) + spread[...] * total).astype(BF16)
+        part = pl.ds(2 * m * levels, 2 * levels)
+        turned = jnp.concatenate([packets[t, part, :] for t in range(sections)], axis=1)
+        terms = dot(turned, grouped[m]).astype(BF16)
+        total = dot(diagonal[...], terms)
+        ready[m] = (control[m].astype(F32) + spread[...] * total).astype(BF16)
         copy = pltpu.make_async_copy(ready.at[m], out.at[m], sems.at[m + 1])
         copy.start()
         leaving.append(copy)
@@ -313,6 +317,7 @@
         scratch_shapes=[
             pltpu.VMEM(control.shape, BF16),
             pltpu.VMEM((sections, slots), F32),
+            pltpu.VMEM((2 * mixing.shape[0], 2 * mixing.shape[0]), BF16),
             pltpu.SemaphoreType.DMA((1 + waves_here,)),
         ],
         name="backward_gradient",
@@ -349,7 +354,9 @@
         grouped = regroup(legendre, sections, bands)
         row_fields, tables, grouped = lax.optimization_barrier((row_fields, tables, grouped))
         by_wave, kern, lines = tables
-        adjoint, pieces = observe(by_wave, row_fields.reshape(terms, levels), kern, lines)
+        adjoint, pieces = observe(
+            by_wave, row_fields.reshape(terms, levels), kern, lines, bands
+        )
         back = lax.all_to_all(
             adjoint.reshape(bands, tile, levels), "band", split_axis=0, concat_axis=0, tiled=True
         )

time: 118 us -> 118 us (level)
  no operation moved by 1% of the time
where the time goes in v4:
time: 118 us; the launch traced here: 117 us
  blocking collectives  66.7 us (57%)
  starting transfers between devices  19 us (16%)
  waiting for transfers between devices  17.2 us (15%)
  Pallas kernels  12.1 us (10%)
  local copies, waits for them, and re-layouts  1.39 us (1%)
    all_to_all x1, blocking collectives, local(): lax.all_to_all(adjoint.reshape(bands, tile, levels), 'band', split_axis=0...  28.8 us
    all_to_all x1, blocking collectives, local(): lax.all_to_all(fields.reshape(sections, bands, tile, levels), 'section',...  19.5 us
    all_to_all x1, starting transfers between devices, local(): lax.all_to_all(field_sum.reshape(bands, tile, levels), 'band', split_axis...  19 us
    all_to_all x1, blocking collectives, local(): lax.all_to_all(pack(back.reshape(terms, levels), pieces, sections, tile),...  18.4 us
    all_to_all x1, waiting for transfers between devices, local(): lax.all_to_all(field_sum.reshape(bands, tile, levels), 'band', split_axis...  17.2 us
    pallas_call x1, Pallas kernels, forward_fields(): pl.pallas_call(functools.partial(forward_body, sections, bands), in_specs...  3.67 us
    pallas_call x1, Pallas kernels, make_basis(): pl.pallas_call(basis_body, in_specs=[SCALAR, SCALAR, WHOLE, WHOLE, WHOLE,...  2.56 us
  transfers between devices with their start and end apart: 1, of which 1 were waited for; matrix products, arithmetic and copies ran while one was open for 0% of the time, Pallas kernels for 3%

profile of v4, /device:TPU:32, one launch (start us, length us, event | category | flops | bytes accessed | tf_op | source)
XLA Modules:
  0.0 117.2 jit_solution(18351183314267850716)
XLA Ops:
  0.6 3.7 %forward_fields.1 = bf16[4096,128]{1,0:T(8,128)(2,1)S(1)} custom-call(bf16[4,256,512]{2,1,0:T(8,128)(2,1)} %bitcast.12, bf16[4,512,512]{2,1,0:T(8,128)(2,1)} %legendre.3, f32[1,512]{1,0:T(1,128)} %spread.3, bf16[128,128]{1,0:T(8,128)(2,1)} %bitcast.17), custom_call_target="tpu_custom_call" | custom-call | tf_op jit(solution)/shard_map/forward_fields/pallas_call | solution.py:112
  4.3 0.0 copy-start
  4.3 19.5 %all_to_all.20 = bf16[4,128,8,128]{3,2,1,0:T(8,128)(2,1)S(1)} all-to-all(bf16[4,128,8,128]{3,2,1,0:T(8,128)(2,1)S(1)} %bitcast.11), channel_id=1, replica_groups=mesh['section'=4,'band'=128] {'section'}, dimensions={0} | all-to-all | bytes 2097152 | tf_op jit(solution)/shard_map/all_to_all | solution.py:342
  23.8 0.8 sum_sections.1
  24.6 19.0 %all-to-all-start.1 = ((bf16[128,8,128]{2,1,0:T(8,128)(2,1)}), bf16[128,8,128]{2,1,0:T(8,128)(2,1)S(1)}, u32[]{:S(2)}, u32[]{:S(2)}) async-start(bf16[128,8,128]{2,1,0:T(8,128)(2,1)} %bitcast.4), calls=%async_computation.1 | async-start | bytes 524288 | tf_op jit(solution)/shard_map/all_to_all | solution.py:347
  43.7 0.0 copy-done
  43.7 0.0 copy-start.5
  43.7 0.0 copy-start.6
  43.7 0.0 copy-start.7
  43.7 0.0 copy-start.9
  43.7 1.3 %regroup.1.grouped = bf16[4,512,512]{2,1,0:T(8,128)(2,1)S(1)} custom-call(bf16[4,512,512]{2,1,0:T(8,128)(2,1)S(1)} %copy-done), custom_call_target="tpu_custom_call" | custom-call | tf_op jit(solution)/shard_map/regroup/pallas_call | solution.py:236
  45.0 0.0 copy-start.1
  45.0 1.3 %copy-done.1 = bf16[4,512,512]{2,1,0:T(8,128)(2,1)} copy-done((bf16[4,512,512]{2,1,0:T(8,128)(2,1)}, bf16[4,512,512]{2,1,0:T(8,128)(2,1)S(1)}, u32[]{:S(2)}) %copy-start.1) | copy-done | bytes 2097176
  46.4 0.0 copy-done.5
  46.4 0.0 copy-done.6
  46.4 0.0 copy-done.7
  46.4 0.0 copy-done.9
  46.4 2.6 %make_basis.1 = (bf16[1024,1024]{1,0:T(8,128)(2,1)S(1)}, bf16[128,1024]{1,0:T(8,128)(2,1)S(1)}, f32[8,1024]{1,0:T(8,128)S(1)}) custom-call(s32[1]{0:T(128)} %bitcast.5.here, s32[4]{0:T(128)S(1)} %copy-done.9, s32[4,1024]{1,0:T(4,128)S(1)} %copy-done.5, f32[4,1024]{1,0:T(4,128)S(1)} %copy-done.6, f32[4,1024]{1,0:T(4,128)S(1)} %copy-done.7, ...), custom_call_target="tpu_custom_call" | custom-call | tf_op jit(solution)/shard_map/make_basis/pallas_call | solution.py:165
  48.9 17.2 %all-to-all-done.1 = bf16[128,8,128]{2,1,0:T(8,128)(2,1)S(1)} async-done(((bf16[128,8,128]{2,1,0:T(8,128)(2,1)}), bf16[128,8,128]{2,1,0:T(8,128)(2,1)S(1)}, u32[]{:S(2)}, u32[]{:S(2)}) %all-to-all-start.1) | async-done | bytes 262176 | tf_op jit(solution)/shard_map/all_to_all | solution.py:347
  66.2 1.3 %observe.1 = (bf16[1024,128]{1,0:T(8,128)(2,1)S(1)}, bf16[24,128]{1,0:T(8,128)(2,1)S(1)}) custom-call(bf16[1024,1024]{1,0:T(8,128)(2,1)S(1)} %get-tuple-element.17.by_wave, bf16[1024,128]{1,0:T(8,128)(2,1)S(1)} %bitcast.15, bf16[128,1024]{1,0:T(8,128)(2,1)S(1)} %get-tuple-element.19.kern, f32[8,1024]{1,0:T(8,128)S(1)} %get-tuple-element.20.lines), custom_call_target="tpu_custom_call" | custom-call | tf_op jit(solution)/shard_map/observe/pallas_call | solution.py:199
  67.5 0.0 copy-start.2
  67.5 0.0 copy-start.3
  67.5 0.0 copy-start.4
  67.5 0.0 copy-start.8
  67.5 28.8 %all_to_all.21 = bf16[128,8,128]{2,1,0:T(8,128)(2,1)S(1)} all-to-all(bf16[128,8,128]{2,1,0:T(8,128)(2,1)S(1)} %bitcast.16), channel_id=1, replica_groups=mesh['section'=4,'band'=128] {'band'}, dimensions={0} | all-to-all | bytes 524288 | tf_op jit(solution)/shard_map/all_to_all | solution.py:360
  96.3 0.2 pack.1
  96.5 18.4 %all_to_all.22.packets = bf16[4,1048,128]{2,1,0:T(8,128)(2,1)S(1)} all-to-all(bf16[4,1048,128]{2,1,0:T(8,128)(2,1)S(1)} %pack.1), channel_id=1, replica_groups=mesh['section'=4,'band'=128] {'section'}, dimensions={0} | all-to-all | bytes 2146304 | tf_op jit(solution)/shard_map/all_to_all | solution.py:363
  114.9 0.0 copy-done.2
  114.9 0.0 copy-done.3
  114.9 0.0 copy-done.4
  114.9 0.0 copy-done.8
  114.9 2.3 %backward_gradient.1 = (bf16[4,256,512]{2,1,0:T(8,128)(2,1)}, f32[4,1024]{1,0:T(4,128)}) custom-call(bf16[4,1048,128]{2,1,0:T(8,128)(2,1)S(1)} %all_to_all.22.packets, bf16[4,512,512]{2,1,0:T(8,128)(2,1)S(1)} %copy-done.2, bf16[4,256,512]{2,1,0:T(8,128)(2,1)S(1)} %bitcast.13, f32[1,512]{1,0:T(1,128)S(1)} %copy-done.8, bf16[128,128]{1,0:T(8,128)(2,1)S(1)} %bitcast.18), custom_call_target="tpu_custom_call" | custom-call | tf_op jit(solution)/shard_map/backward_gradient/pallas_call | solution.py:309
Async XLA Ops:
  4.3 39.4 %copy-start = (bf16[4,512,512]{2,1,0:T(8,128)(2,1)S(1)}, bf16[4,512,512]{2,1,0:T(8,128)(2,1)}, u32[]{:S(2)}) copy-start(bf16[4,512,512]{2,1,0:T(8,128)(2,1)} %legendre.3) | copy-start | bytes 6291460
  24.6 41.5 %all-to-all-start.1 = ((bf16[128,8,128]{2,1,0:T(8,128)(2,1)}), bf16[128,8,128]{2,1,0:T(8,128)(2,1)S(1)}, u32[]{:S(2)}, u32[]{:S(2)}) async-start(bf16[128,8,128]{2,1,0:T(8,128)(2,1)} %bitcast.4), calls=%async_computation.1 | async-start | bytes 524288 | tf_op jit(solution)/shard_map/all_to_all | solution.py:347
  43.7 2.7 %copy-start.5 = (s32[4,1024]{1,0:T(4,128)S(1)}, s32[4,1024]{1,0:T(4,128)}, u32[]{:S(2)}) copy-start(s32[4,1024]{1,0:T(4,128)} %obs_lon.1) | copy-start | bytes 49156
  43.7 2.7 %copy-start.6 = (f32[4,1024]{1,0:T(4,128)S(1)}, f32[4,1024]{1,0:T(4,128)}, u32[]{:S(2)}) copy-start(f32[4,1024]{1,0:T(4,128)} %value.1) | copy-start | bytes 49156
  43.7 2.7 %copy-start.7 = (f32[4,1024]{1,0:T(4,128)S(1)}, f32[4,1024]{1,0:T(4,128)}, u32[]{:S(2)}) copy-start(f32[4,1024]{1,0:T(4,128)} %weight.1) | copy-start | bytes 49156
  43.7 2.7 %copy-start.9 = (s32[4]{0:T(128)S(1)}, s32[4]{0:T(128)}, u32[]{:S(2)}) copy-start(s32[4]{0:T(128)} %count.1) | copy-start | bytes 52
  45.0 1.3 %copy-start.1 = (bf16[4,512,512]{2,1,0:T(8,128)(2,1)}, bf16[4,512,512]{2,1,0:T(8,128)(2,1)S(1)}, u32[]{:S(2)}) copy-start(bf16[4,512,512]{2,1,0:T(8,128)(2,1)S(1)} %regroup.1.grouped) | copy-start | bytes 6291460
  67.5 47.4 %copy-start.2 = (bf16[4,512,512]{2,1,0:T(8,128)(2,1)S(1)}, bf16[4,512,512]{2,1,0:T(8,128)(2,1)}, u32[]{:S(2)}) copy-start(bf16[4,512,512]{2,1,0:T(8,128)(2,1)} %copy-done.1) | copy-start | bytes 6291460
  67.5 47.4 %copy-start.3 = (bf16[1,4,2,128,512]{4,3,2,1,0:T(8,128)(2,1)S(1)}, bf16[1,4,2,128,512]{4,3,2,1,0:T(8,128)(2,1)}, u32[]{:S(2)}) copy-start(bf16[1,4,2,128,512]{4,3,2,1,0:T(8,128)(2,1)} %param.9) | copy-start | bytes 3145732
  67.5 47.4 %copy-start.4 = (bf16[1,128,128]{2,1,0:T(8,128)(2,1)S(1)}, bf16[1,128,128]{2,1,0:T(8,128)(2,1)}, u32[]{:S(2)}) copy-start(bf16[1,128,128]{2,1,0:T(8,128)(2,1)} %param.12) | copy-start | bytes 98308
  67.5 47.4 %copy-start.8 = (f32[1,512]{1,0:T(1,128)S(1)}, f32[1,512]{1,0:T(1,128)}, u32[]{:S(2)}) copy-start(f32[1,512]{1,0:T(1,128)} %spread.3) | copy-start | bytes 6148

commit v5 on v3

v5 whole, which is shorter than its diff:
```python
import functools
import math

import jax
import jax.numpy as jnp
from jax import lax
from jax.experimental import pallas as pl
from jax.experimental.pallas import tpu as pltpu
from jax.sharding import Mesh
from jax.sharding import PartitionSpec as P

NLON = 1024
BAND = ("z", "x", "core")
F32 = jnp.float32
BF16 = jnp.bfloat16
MINOR_BOTH = (((1,), (1,)), ((), ()))


WHOLE = pl.BlockSpec(memory_space=pltpu.VMEM)
SCALAR = pl.BlockSpec(memory_space=pltpu.SMEM)
APART = pl.BlockSpec(memory_space=pl.ANY)


LIMIT = pltpu.CompilerParams(vmem_limit_bytes=16 << 20)


def made(shape, kind):
    return pltpu.VMEM(shape, kind)


def near(array):
    return pltpu.with_memory_space_constraint(array, pltpu.VMEM)


def view(ref, shape):
    return ref.reshape(shape)


def far(array):
    return pltpu.with_memory_space_constraint(array, pltpu.HBM)


def dot(a, b):
    return jnp.dot(a, b, preferred_element_type=F32)


def dot_minor(a, b):
    return lax.dot_general(a, b, MINOR_BOTH, preferred_element_type=F32)


def grouping(grid):
    sections, z, x, cores = grid
    bands = z * x * cores
    size = sections * bands
    place = lax.broadcasted_iota(jnp.int32, (size, size), 0)
    row = lax.broadcasted_iota(jnp.int32, (size, size), 1)
    band = (place // cores % z * x + place // (cores * z) % x) * cores + place % cores
    return jnp.where(sections * band + place // bands == row, 1.0, 0.0).astype(BF16)


def pull(pairs, sems):
    copies = [pltpu.make_async_copy(a, b, sems.at[i]) for i, (a, b) in enumerate(pairs)]
    for copy in copies:
        copy.start()
    return copies


def forward_body(
    grid, control, legendre, spread, mixing, out,
    held, coeffs, basis, spreads, mixings, diagonal, sems,
):
    waves_here, pairs, _ = control.shape
    levels = mixing.shape[0]
    latitudes = legendre.shape[2]
    tile = 2 * waves_here
    order = [(spread, spreads), (mixing, mixings)]
    for m in range(waves_here):
        order += [(control.at[m], coeffs.at[m]), (legendre.at[m], basis.at[m])]
    copies = [pltpu.make_async_copy(a, b, sems.at[i]) for i, (a, b) in enumerate(order)]
    for copy in copies[:6]:
        copy.start()
    copies[0].wait()
    copies[1].wait()
    diagonal[...] = jnp.zeros_like(diagonal)
    for r in range(2):
        part = pl.ds(r * levels, levels)
        diagonal[part, part] = mixings[...]
    for m in range(waves_here):
        copies[2 + 2 * m].wait()
        copies[3 + 2 * m].wait()
        for copy in copies[6 + 2 * m : 8 + 2 * m]:
            copy.start()
        scaled = (coeffs[m].astype(F32) * spreads[...]).astype(BF16)
        rows = lax.dot_general(
            basis[m], scaled, (((0,), (1,)), ((), ())), preferred_element_type=F32
        ).astype(BF16)
        fields = dot_minor(rows, diagonal[...])
        for r in range(2):
            held[pl.ds(2 * m + r, latitudes, stride=tile), :] = fields[
                :, r * levels : (r + 1) * levels
            ]
    sections, z, x, cores = grid
    placed = view(held, (z, x, cores, sections, tile, levels))
    size = z * cores * tile
    for t in range(sections):
        for i in range(x):
            block = placed[:, i, :, t].reshape(size, levels)
            out[pl.ds((t * x + i) * size, size), :] = block.astype(BF16)


def forward_fields(control, legendre, spread, mixing, grid):
    waves_here, pairs, numbers = control.shape
    latitudes = legendre.shape[2]
    levels = mixing.shape[0]
    rows = latitudes * 2 * waves_here
    return pl.pallas_call(
        functools.partial(forward_body, grid),
        in_specs=[APART] * 4,
        out_specs=WHOLE,
        out_shape=made((rows, levels), BF16),
        scratch_shapes=[
            pltpu.VMEM((rows, levels), F32),
            pltpu.VMEM(control.shape, BF16),
            pltpu.VMEM(legendre.shape, BF16),
            pltpu.VMEM(spread.shape, F32),
            pltpu.VMEM(mixing.shape, BF16),
            pltpu.VMEM((2 * levels, 2 * levels), BF16),
            pltpu.SemaphoreType.DMA((2 + 2 * waves_here,)),
        ],
        name="forward_fields",
        compiler_params=LIMIT,
    )(far(control), far(legendre), far(spread), far(mixing))


def turn(index):
    angle = (index & (NLON - 1)).astype(F32) * (2.0 * math.pi / NLON)
    return jnp.cos(angle), jnp.sin(angle)


def basis_body(
    grid, tile, here, at_x, count, obs_lon, value, weight, kernels, by_wave, turned, lines, kern, sems
):
    copy = pull([(kernels.at[here[0]], kern)], sems)[0]
    terms, slots = by_wave.shape
    line = pl.ds(here[0], 1)
    lon = obs_lon[line, :]
    _, z, x, cores = grid
    run = x * cores * tile
    fine = lax.broadcasted_iota(jnp.int32, (run, 1), 0)
    band = (fine // tile) % x * cores + fine // (tile * x)
    wave = band * (tile // 2) + fine % tile // 2
    fine_cos, fine_sin = turn(wave * lon + fine % 2 * (NLON // 4))
    coarse = lax.broadcasted_iota(jnp.int32, (z, 1), 0)
    coarse_cos, coarse_sin = turn(coarse * (run // 2) * lon)
    coarse_cos, coarse_sin = 2.0 * coarse_cos, 2.0 * coarse_sin
    for a in range(z):
        block = coarse_cos[a : a + 1] * fine_cos - coarse_sin[a : a + 1] * fine_sin
        if a == 0:
            block = jnp.where(fine < 2, fine_cos, block)
        by_wave[pl.ds(a * run, run), :] = block.astype(BF16)
    slot = lax.broadcasted_iota(jnp.int32, (1, slots), 1)
    lines[pl.ds(0, 1), :] = value[line, :]
    lines[pl.ds(1, 1), :] = weight[line, :]
    lines[pl.ds(2, 1), :] = jnp.where(slot < count[here[0]], 1.0, 0.0)
    for i in range(x):
        flag = jnp.where(at_x[0] == i, 1.0, 0.0)
        lines[pl.ds(3 + i, 1), :] = jnp.full((1, slots), flag, F32)
    levels = kern.shape[1]
    eye = lax.broadcasted_iota(jnp.int32, (levels, levels), 0) == lax.broadcasted_iota(
        jnp.int32, (levels, levels), 1
    )
    copy.wait()
    turned[...] = dot_minor(jnp.where(eye, 1.0, 0.0).astype(BF16), kern[...]).astype(BF16)


def make_basis(here, at_x, count, obs_lon, value, weight, kernels, terms, grid, tile):
    _, slots, levels = kernels.shape
    return pl.pallas_call(
        functools.partial(basis_body, grid, tile),
        in_specs=[SCALAR, SCALAR, SCALAR, WHOLE, WHOLE, WHOLE, APART],
        out_specs=[WHOLE] * 3,
        out_shape=[
            made((terms, slots), BF16),
            made((levels, slots), BF16),
            made((8, slots), F32),
        ],
        scratch_shapes=[pltpu.VMEM((slots, levels), BF16), pltpu.SemaphoreType.DMA((1,))],
        name="make_basis",
        compiler_params=LIMIT,
    )(here, at_x, count, obs_lon, value, weight, far(kernels))


def observe_body(by_wave, fields, kern, lines, adjoint, pieces, departures):
    columns = dot(fields[...].T, by_wave[...])
    wide = kern[...].astype(F32)
    evolved = jnp.sum(wide * columns, axis=0, keepdims=True)
    departed = jnp.where(lines[pl.ds(2, 1), :] > 0.5, evolved - lines[pl.ds(0, 1), :], 0.0)
    scaled = (lines[pl.ds(1, 1), :] * departed * wide).astype(BF16)
    adjoint[...] = dot_minor(scaled, by_wave[...]).T.astype(BF16)
    size, lanes = departures.shape
    for i in range(size):
        departures[pl.ds(i, 1), :] = departed[:, i * lanes : (i + 1) * lanes]
    rest = departures[...]
    for i in range(3):
        piece = rest.astype(BF16)
        pieces[pl.ds(i * size, size), :] = piece
        rest = rest - piece.astype(F32)


def observe(by_wave, fields, kern, lines):
    levels, slots = kern.shape
    return pl.pallas_call(
        observe_body,
        in_specs=[WHOLE] * 4,
        out_specs=[WHOLE, WHOLE],
        out_shape=[made(fields.shape, BF16), made((3 * slots // levels, levels), BF16)],
        scratch_shapes=[pltpu.VMEM((slots // levels, levels), F32)],
        name="observe",
        compiler_params=LIMIT,
    )(near(by_wave), near(fields), near(kern), near(lines))


def sum_body(parts, out):
    sections, places = parts.shape[:2]
    for i in range(places):
        total = parts[0, i].astype(F32)
        for section in range(1, sections):
            total = total + parts[section, i].astype(F32)
        out[:, i] = total.astype(BF16)


def sum_sections(parts):
    _, places, groups, tile, levels = parts.shape
    return pl.pallas_call(
        sum_body,
        in_specs=[WHOLE],
        out_specs=WHOLE,
        out_shape=made((groups, places, tile, levels), BF16),
        name="sum_sections",
        compiler_params=LIMIT,
    )(near(parts))


def regroup_body(grid, legendre, out):
    group = grouping(grid)
    for m in range(legendre.shape[0]):
        out[m] = dot_minor(group, legendre[m]).astype(BF16)


def regroup(legendre, grid):
    waves_here, numbers, latitudes = legendre.shape
    return pl.pallas_call(
        functools.partial(regroup_body, grid),
        in_specs=[WHOLE],
        out_specs=WHOLE,
        out_shape=jax.ShapeDtypeStruct((waves_here, latitudes, numbers), BF16),
        name="regroup",
        compiler_params=LIMIT,
    )(legendre)


def pack_body(grid, tile, body, pieces, lines, out, held):
    sections, z, x, cores = grid
    held[...] = body[...].astype(F32)
    run = z * cores
    whole = pieces[...].astype(F32)
    for place in range(x):
        for i in range(tile):
            block = held[pl.ds(place * tile + i, run, stride=x * tile), :].astype(BF16)
            for section in range(sections):
                out[section * x + place, pl.ds(i * run, run), :] = block
        own = (whole * lines[pl.ds(3 + place, 1), pl.ds(0, whole.shape[1])]).astype(BF16)
        for section in range(sections):
            out[section * x + place, pl.ds(tile * run, whole.shape[0]), :] = own


def pack(body, pieces, lines, grid, tile):
    sections, z, x, cores = grid
    rows = tile * z * cores + pieces.shape[0]
    return pl.pallas_call(
        functools.partial(pack_body, grid, tile),
        in_specs=[WHOLE, WHOLE, WHOLE],
        out_specs=WHOLE,
        out_shape=made((sections * x, rows, body.shape[1]), BF16),
        scratch_shapes=[pltpu.VMEM(body.shape, F32)],
        name="pack",
        compiler_params=LIMIT,
    )(near(body), near(pieces), near(lines))


def backward_body(
    packets, grouped, control, spread, mixing, out, all_departures,
    ready, departures, diagonal, sems,
):
    origins, _, levels = packets.shape
    waves_here = grouped.shape[0]
    run = grouped.shape[1] // origins
    size = run * 2 * waves_here
    count = departures.shape[1] // levels
    sections = departures.shape[0]
    x = origins // sections
    for t in range(sections):
        parts = []
        for i in range(3):
            part = pl.ds(size + i * count, count)
            own = [packets[t * x + place, part, :].astype(F32) for place in range(x)]
            parts.append(sum(own[1:], own[0]))
        whole = (parts[2] + parts[1]) + parts[0]
        for i in range(count):
            departures[pl.ds(t, 1), pl.ds(i * levels, levels)] = whole[i : i + 1]
    leaving = pull([(departures, all_departures)], sems)
    mixing_t = mixing[...].astype(F32).T.astype(BF16)
    diagonal[...] = jnp.zeros_like(diagonal)
    for r in range(2):
        part = pl.ds(r * levels, levels)
        diagonal[part, part] = mixing_t
    for m in range(waves_here):
        rows = [
            jnp.concatenate([packets[t, pl.ds((2 * m + r) * run, run), :] for t in range(origins)])
            for r in range(2)
        ]
        terms = lax.dot_general(
            jnp.concatenate(rows, axis=1), grouped[m], (((0,), (0,)), ((), ())),
            preferred_element_type=F32,
        ).astype(BF16)
        total = dot(diagonal[...], terms)
        ready[m] = (control[m].astype(F32) + spread[...] * total).astype(BF16)
        copy = pltpu.make_async_copy(ready.at[m], out.at[m], sems.at[m + 1])
        copy.start()
        leaving.append(copy)
    for copy in leaving:
        copy.wait()


def backward_gradient(packets, grouped, control, spread, mixing, sections, slots):
    waves_here = grouped.shape[0]
    return pl.pallas_call(
        backward_body,
        in_specs=[WHOLE] * 5,
        out_specs=[APART, APART],
        out_shape=[
            jax.ShapeDtypeStruct(control.shape, BF16),
            jax.ShapeDtypeStruct((sections, slots), F32),
        ],
        scratch_shapes=[
            pltpu.VMEM(control.shape, BF16),
            pltpu.VMEM((sections, slots), F32),
            pltpu.VMEM((2 * mixing.shape[0], 2 * mixing.shape[0]), BF16),
            pltpu.SemaphoreType.DMA((1 + waves_here,)),
        ],
        name="backward_gradient",
        compiler_params=LIMIT,
    )(near(packets), near(grouped), near(control), near(spread), near(mixing))


def make_local(grid):
    sections, z, x, cores = grid
    bands = z * x * cores

    def local(
        control, legendre, spectral_sd, vertical, obs_lon, obs_count, kernels, obs_value, obs_weight
    ):
        mixing = vertical[0]
        waves_here, numbers, latitudes = legendre.shape
        levels = mixing.shape[0]
        tile = 2 * waves_here
        terms = tile * bands
        slots = obs_lon.shape[1]
        here = lax.axis_index("section").astype(jnp.int32)
        coeffs = control.reshape(waves_here, 2 * levels, numbers)

        fields = forward_fields(coeffs, legendre, spectral_sd, mixing, grid)
        shares = lax.all_to_all(
            fields.reshape(sections * x, z * cores, tile, levels),
            ("section", "x"), split_axis=0, concat_axis=0, tiled=True,
        )
        field_sum = sum_sections(shares.reshape(sections, x, z * cores, tile, levels))
        row_fields = lax.all_to_all(
            field_sum, ("z", "core"), split_axis=0, concat_axis=0, tiled=True
        )
        at_x = lax.axis_index("x").astype(jnp.int32)
        tables = make_basis(
            here[None], at_x[None], obs_count, obs_lon, obs_value, obs_weight, kernels,
            terms, grid, tile,
        )
        grouped = regroup(legendre, grid)
        row_fields, tables, grouped = lax.optimization_barrier((row_fields, tables, grouped))
        by_wave, kern, lines = tables
        adjoint, pieces = observe(by_wave, row_fields.reshape(terms, levels), kern, lines)
        back = lax.all_to_all(
            adjoint.reshape(z * cores, x, tile, levels),
            ("z", "core"), split_axis=0, concat_axis=0, tiled=True,
        )
        packets = lax.all_to_all(
            pack(back.reshape(terms, levels), pieces, lines, grid, tile),
            ("section", "x"), split_axis=0, concat_axis=0, tiled=True,
        )
        gradient, all_departures = backward_gradient(
            packets, grouped, coeffs, spectral_sd, mixing, sections, slots
        )
        return (gradient.reshape(control.shape), all_departures)

    return local


def solution(mesh):
    sections, bands = mesh.shape["section"], mesh.shape["band"]
    cores = 2
    x = min(4, bands // cores)
    z = bands // (cores * x)
    fine_mesh = Mesh(mesh.devices.reshape(sections, z, x, cores), ("section",) + BAND)
    in_specs = (
        P("section", BAND, None, None, None),
        P(BAND, None, None),
        P("section", None),
        P("section", None, None),
        P(BAND, None),
        P(BAND),
        P(BAND, None, None),
        P(BAND, None),
        P(BAND, None),
    )
    out_specs = (P("section", BAND, None, None, None), P(BAND, None))
    local = make_local((sections, z, x, cores))
    return jax.shard_map(
        local, mesh=fine_mesh, in_specs=in_specs, out_specs=out_specs, check_vma=False
    )
```

time: 118 us -> 117 us (level)
  the two profiles are of different devices: /device:TPU:32 before, /device:TPU:2 now
where the time goes in v5:
time: 117 us
  blocking collectives  69.7 us (60%)
  waiting for transfers between devices  17.4 us (15%)
  starting transfers between devices  15.4 us (13%)
  Pallas kernels  12.4 us (11%)
  local copies, waits for them, and re-layouts  1.39 us (1%)
    all_to_all x1, blocking collectives, local(): lax.all_to_all(adjoint.reshape(z * cores, x, tile, levels), ('z', 'core')...  26 us
    all_to_all x1, blocking collectives, local(): lax.all_to_all(fields.reshape(sections * x, z * cores, tile, levels), ('s...  23.3 us
    all_to_all x1, blocking collectives, local(): lax.all_to_all(pack(back.reshape(terms, levels), pieces, lines, grid, til...  20.4 us
    all_to_all x1, waiting for transfers between devices, local(): lax.all_to_all(field_sum, ('z', 'core'), split_axis=0, concat_axis=0, til...  17.4 us
    all_to_all x1, starting transfers between devices, local(): lax.all_to_all(field_sum, ('z', 'core'), split_axis=0, concat_axis=0, til...  15.4 us
    pallas_call x1, Pallas kernels, forward_fields(): pl.pallas_call(functools.partial(forward_body, grid), in_specs=[APART] *...  3.7 us
    pallas_call x1, Pallas kernels, make_basis(): pl.pallas_call(functools.partial(basis_body, grid, tile), in_specs=[SCALA...  2.57 us
  transfers between devices with their start and end apart: 1, of which 1 were waited for; matrix products, arithmetic and copies ran while one was open for 0% of the time, Pallas kernels for 3%

profile of v5, /device:TPU:2, one launch (start us, length us, event | category | flops | bytes accessed | tf_op | source)
XLA Modules:
  0.0 117.1 jit_solution(16283231218826985218)
XLA Ops:
  0.6 3.7 %forward_fields.1 = bf16[4096,128]{1,0:T(8,128)(2,1)S(1)} custom-call(bf16[4,256,512]{2,1,0:T(8,128)(2,1)} %bitcast.12, bf16[4,512,512]{2,1,0:T(8,128)(2,1)} %legendre.3, f32[1,512]{1,0:T(1,128)} %spread.3, bf16[128,128]{1,0:T(8,128)(2,1)} %bitcast.17), custom_call_target="tpu_custom_call" | custom-call | tf_op jit(solution)/shard_map/forward_fields/pallas_call | solution.py:116
  4.3 0.0 copy-start
  4.3 23.3 %all_to_all.20 = bf16[16,32,8,128]{3,2,1,0:T(8,128)(2,1)S(1)} all-to-all(bf16[16,32,8,128]{3,2,1,0:T(8,128)(2,1)S(1)} %bitcast.11), channel_id=1, replica_groups=mesh['section'=4,'z'=16,'x'=4,'core'=2] {'section','x'}, dimensions={0} | all-to-all | bytes 2097152 | tf_op jit(solution)/shard_map/all_to_all | solution.py:373
  27.6 0.8 sum_sections.1
  28.5 15.4 %all-to-all-start.1 = ((bf16[32,4,8,128]{3,2,1,0:T(8,128)(2,1)}), bf16[32,4,8,128]{3,2,1,0:T(8,128)(2,1)S(1)}, u32[]{:S(2)}, u32[]{:S(2)}) async-start(bf16[32,4,8,128]{3,2,1,0:T(8,128)(2,1)} %sum_sections.1), calls=%async_computation.1 | async-start | bytes 524288 | tf_op jit(solution)/shard_map/all_to_all | solution.py:378
  43.9 0.0 copy-done
  43.9 0.0 copy-start.5
  43.9 0.0 copy-start.6
  43.9 0.0 copy-start.7
  43.9 0.0 copy-start.9
  43.9 1.3 %regroup.1.grouped = bf16[4,512,512]{2,1,0:T(8,128)(2,1)S(1)} custom-call(bf16[4,512,512]{2,1,0:T(8,128)(2,1)S(1)} %copy-done), custom_call_target="tpu_custom_call" | custom-call | tf_op jit(solution)/shard_map/regroup/pallas_call | solution.py:252
  45.2 0.0 copy-start.1
  45.3 1.3 %copy-done.1 = bf16[4,512,512]{2,1,0:T(8,128)(2,1)} copy-done((bf16[4,512,512]{2,1,0:T(8,128)(2,1)}, bf16[4,512,512]{2,1,0:T(8,128)(2,1)S(1)}, u32[]{:S(2)}) %copy-start.1) | copy-done | bytes 2097176
  46.6 0.0 copy-done.5
  46.6 0.0 copy-done.6
  46.6 0.0 copy-done.7
  46.6 0.0 copy-done.9
  46.6 2.6 %make_basis.1 = (bf16[1024,1024]{1,0:T(8,128)(2,1)S(1)}, bf16[128,1024]{1,0:T(8,128)(2,1)S(1)}, f32[8,1024]{1,0:T(8,128)S(1)}) custom-call(s32[1]{0:T(128)} %bitcast.4.here, s32[1]{0:T(128)} %bitcast.5.at_x, s32[4]{0:T(128)S(1)} %copy-done.9, s32[4,1024]{1,0:T(4,128)S(1)} %copy-done.5, f32[4,1024]{1,0:T(4,128)S(1)} %copy-done.6, f32[4,1024]{1,0:T(4,128)S(1)} %copy-done.7, ...), custom_call_target="tpu_custom_call" | custom-call | tf_op jit(solution)/shard_map/make_basis/pallas_call | solution.py:178
  49.2 17.4 %all-to-all-done.1 = bf16[32,4,8,128]{3,2,1,0:T(8,128)(2,1)S(1)} async-done(((bf16[32,4,8,128]{3,2,1,0:T(8,128)(2,1)}), bf16[32,4,8,128]{3,2,1,0:T(8,128)(2,1)S(1)}, u32[]{:S(2)}, u32[]{:S(2)}) %all-to-all-start.1) | async-done | bytes 262176 | tf_op jit(solution)/shard_map/all_to_all | solution.py:378
  66.6 1.3 %observe.1 = (bf16[1024,128]{1,0:T(8,128)(2,1)S(1)}, bf16[24,128]{1,0:T(8,128)(2,1)S(1)}) custom-call(bf16[1024,1024]{1,0:T(8,128)(2,1)S(1)} %get-tuple-element.17.by_wave, bf16[1024,128]{1,0:T(8,128)(2,1)S(1)} %bitcast.15, bf16[128,1024]{1,0:T(8,128)(2,1)S(1)} %get-tuple-element.19.kern, f32[8,1024]{1,0:T(8,128)S(1)} %get-tuple-element.20.lines), custom_call_target="tpu_custom_call" | custom-call | tf_op jit(solution)/shard_map/observe/pallas_call | solution.py:212
  67.9 0.0 copy-start.2
  67.9 0.0 copy-start.3
  67.9 0.0 copy-start.4
  67.9 0.0 copy-start.8
  67.9 26.0 %all_to_all.21 = bf16[32,4,8,128]{3,2,1,0:T(8,128)(2,1)S(1)} all-to-all(bf16[32,4,8,128]{3,2,1,0:T(8,128)(2,1)S(1)} %bitcast.16), channel_id=1, replica_groups=mesh['section'=4,'z'=16,'x'=4,'core'=2] {'z','core'}, dimensions={0} | all-to-all | bytes 524288 | tf_op jit(solution)/shard_map/all_to_all | solution.py:390
  93.9 0.4 pack.1
  94.3 20.4 %all_to_all.22.packets = bf16[16,280,128]{2,1,0:T(8,128)(2,1)S(1)} all-to-all(bf16[16,280,128]{2,1,0:T(8,128)(2,1)S(1)} %pack.1), channel_id=1, replica_groups=mesh['section'=4,'z'=16,'x'=4,'core'=2] {'section','x'}, dimensions={0} | all-to-all | bytes 2293760 | tf_op jit(solution)/shard_map/all_to_all | solution.py:394
  114.7 0.0 copy-done.2
  114.7 0.0 copy-done.3
  114.7 0.0 copy-done.4
  114.8 0.0 copy-done.8
  114.8 2.3 %backward_gradient.1 = (bf16[4,256,512]{2,1,0:T(8,128)(2,1)}, f32[4,1024]{1,0:T(4,128)}) custom-call(bf16[16,280,128]{2,1,0:T(8,128)(2,1)S(1)} %all_to_all.22.packets, bf16[4,512,512]{2,1,0:T(8,128)(2,1)S(1)} %copy-done.2, bf16[4,256,512]{2,1,0:T(8,128)(2,1)S(1)} %bitcast.13, f32[1,512]{1,0:T(1,128)S(1)} %copy-done.8, bf16[128,128]{1,0:T(8,128)(2,1)S(1)} %bitcast.18), custom_call_target="tpu_custom_call" | custom-call | tf_op jit(solution)/shard_map/backward_gradient/pallas_call | solution.py:337
Async XLA Ops:
  4.3 39.5 %copy-start = (bf16[4,512,512]{2,1,0:T(8,128)(2,1)S(1)}, bf16[4,512,512]{2,1,0:T(8,128)(2,1)}, u32[]{:S(2)}) copy-start(bf16[4,512,512]{2,1,0:T(8,128)(2,1)} %legendre.3) | copy-start | bytes 6291460
  28.5 38.1 %all-to-all-start.1 = ((bf16[32,4,8,128]{3,2,1,0:T(8,128)(2,1)}), bf16[32,4,8,128]{3,2,1,0:T(8,128)(2,1)S(1)}, u32[]{:S(2)}, u32[]{:S(2)}) async-start(bf16[32,4,8,128]{3,2,1,0:T(8,128)(2,1)} %sum_sections.1), calls=%async_computation.1 | async-start | bytes 524288 | tf_op jit(solution)/shard_map/all_to_all | solution.py:378
  43.9 2.7 %copy-start.5 = (s32[4,1024]{1,0:T(4,128)S(1)}, s32[4,1024]{1,0:T(4,128)}, u32[]{:S(2)}) copy-start(s32[4,1024]{1,0:T(4,128)} %obs_lon.1) | copy-start | bytes 49156
  43.9 2.7 %copy-start.6 = (f32[4,1024]{1,0:T(4,128)S(1)}, f32[4,1024]{1,0:T(4,128)}, u32[]{:S(2)}) copy-start(f32[4,1024]{1,0:T(4,128)} %value.1) | copy-start | bytes 49156
  43.9 2.7 %copy-start.7 = (f32[4,1024]{1,0:T(4,128)S(1)}, f32[4,1024]{1,0:T(4,128)}, u32[]{:S(2)}) copy-start(f32[4,1024]{1,0:T(4,128)} %weight.1) | copy-start | bytes 49156
  43.9 2.7 %copy-start.9 = (s32[4]{0:T(128)S(1)}, s32[4]{0:T(128)}, u32[]{:S(2)}) copy-start(s32[4]{0:T(128)} %count.1) | copy-start | bytes 52
  45.2 1.3 %copy-start.1 = (bf16[4,512,512]{2,1,0:T(8,128)(2,1)}, bf16[4,512,512]{2,1,0:T(8,128)(2,1)S(1)}, u32[]{:S(2)}) copy-start(bf16[4,512,512]{2,1,0:T(8,128)(2,1)S(1)} %regroup.1.grouped) | copy-start | bytes 6291460
  67.9 46.9 %copy-start.2 = (bf16[4,512,512]{2,1,0:T(8,128)(2,1)S(1)}, bf16[4,512,512]{2,1,0:T(8,128)(2,1)}, u32[]{:S(2)}) copy-start(bf16[4,512,512]{2,1,0:T(8,128)(2,1)} %copy-done.1) | copy-start | bytes 6291460
  67.9 46.9 %copy-start.3 = (bf16[1,4,2,128,512]{4,3,2,1,0:T(8,128)(2,1)S(1)}, bf16[1,4,2,128,512]{4,3,2,1,0:T(8,128)(2,1)}, u32[]{:S(2)}) copy-start(bf16[1,4,2,128,512]{4,3,2,1,0:T(8,128)(2,1)} %param.9) | copy-start | bytes 3145732
  67.9 46.9 %copy-start.4 = (bf16[1,128,128]{2,1,0:T(8,128)(2,1)S(1)}, bf16[1,128,128]{2,1,0:T(8,128)(2,1)}, u32[]{:S(2)}) copy-start(bf16[1,128,128]{2,1,0:T(8,128)(2,1)} %param.12) | copy-start | bytes 98308
  67.9 46.9 %copy-start.8 = (f32[1,512]{1,0:T(1,128)S(1)}, f32[1,512]{1,0:T(1,128)}, u32[]{:S(2)}) copy-start(f32[1,512]{1,0:T(1,128)} %spread.3) | copy-start | bytes 6148

commit v6 on v5

--- a/solution.py
+++ b/solution.py
@@ -299,16 +299,7 @@
     count = departures.shape[1] // levels
     sections = departures.shape[0]
     x = origins // sections
-    for t in range(sections):
-        parts = []
-        for i in range(3):
-            part = pl.ds(size + i * count, count)
-            own = [packets[t * x + place, part, :].astype(F32) for place in range(x)]
-            parts.append(sum(own[1:], own[0]))
-        whole = (parts[2] + parts[1]) + parts[0]
-        for i in range(count):
-            departures[pl.ds(t, 1), pl.ds(i * levels, levels)] = whole[i : i + 1]
-    leaving = pull([(departures, all_departures)], sems)
+    leaving = []
     mixing_t = mixing[...].astype(F32).T.astype(BF16)
     diagonal[...] = jnp.zeros_like(diagonal)
     for r in range(2):
@@ -328,6 +319,17 @@
         copy = pltpu.make_async_copy(ready.at[m], out.at[m], sems.at[m + 1])
         copy.start()
         leaving.append(copy)
+        if m == 0:
+            for t in range(sections):
+                parts = []
+                for i in range(3):
+                    part = pl.ds(size + i * count, count)
+                    own = [packets[t * x + place, part, :].astype(F32) for place in range(x)]
+                    parts.append(sum(own[1:], own[0]))
+                whole = (parts[2] + parts[1]) + parts[0]
+                for i in range(count):
+                    departures[pl.ds(t, 1), pl.ds(i * levels, levels)] = whole[i : i + 1]
+            leaving += pull([(departures, all_departures)], sems)
     for copy in leaving:
         copy.wait()
 

time: 117 us -> 117 us (level)
  no operation moved by 1% of the time
where the time goes in v6:
time: 117 us
  blocking collectives  69.7 us (60%)
  waiting for transfers between devices  17.4 us (15%)
  starting transfers between devices  15.4 us (13%)
  Pallas kernels  12.4 us (11%)
  local copies, waits for them, and re-layouts  1.39 us (1%)
    all_to_all x1, blocking collectives, local(): lax.all_to_all(adjoint.reshape(z * cores, x, tile, levels), ('z', 'core')...  26 us
    all_to_all x1, blocking collectives, local(): lax.all_to_all(fields.reshape(sections * x, z * cores, tile, levels), ('s...  23.3 us
    all_to_all x1, blocking collectives, local(): lax.all_to_all(pack(back.reshape(terms, levels), pieces, lines, grid, til...  20.4 us
    all_to_all x1, waiting for transfers between devices, local(): lax.all_to_all(field_sum, ('z', 'core'), split_axis=0, concat_axis=0, til...  17.4 us
    all_to_all x1, starting transfers between devices, local(): lax.all_to_all(field_sum, ('z', 'core'), split_axis=0, concat_axis=0, til...  15.4 us
    pallas_call x1, Pallas kernels, forward_fields(): pl.pallas_call(functools.partial(forward_body, grid), in_specs=[APART] *...  3.7 us
    pallas_call x1, Pallas kernels, make_basis(): pl.pallas_call(functools.partial(basis_body, grid, tile), in_specs=[SCALA...  2.57 us
  transfers between devices with their start and end apart: 1, of which 1 were waited for; matrix products, arithmetic and copies ran while one was open for 0% of the time, Pallas kernels for 3%

profile of v6, /device:TPU:2, one launch (start us, length us, event | category | flops | bytes accessed | tf_op | source)
XLA Modules:
  0.0 117.1 jit_solution(18086717892105390749)
XLA Ops:
  0.6 3.7 %forward_fields.1 = bf16[4096,128]{1,0:T(8,128)(2,1)S(1)} custom-call(bf16[4,256,512]{2,1,0:T(8,128)(2,1)} %bitcast.12, bf16[4,512,512]{2,1,0:T(8,128)(2,1)} %legendre.3, f32[1,512]{1,0:T(1,128)} %spread.3, bf16[128,128]{1,0:T(8,128)(2,1)} %bitcast.17), custom_call_target="tpu_custom_call" | custom-call | tf_op jit(solution)/shard_map/forward_fields/pallas_call | solution.py:116
  4.3 0.0 copy-start
  4.3 23.3 %all_to_all.20 = bf16[16,32,8,128]{3,2,1,0:T(8,128)(2,1)S(1)} all-to-all(bf16[16,32,8,128]{3,2,1,0:T(8,128)(2,1)S(1)} %bitcast.11), channel_id=1, replica_groups=mesh['section'=4,'z'=16,'x'=4,'core'=2] {'section','x'}, dimensions={0} | all-to-all | bytes 2097152 | tf_op jit(solution)/shard_map/all_to_all | solution.py:375
  27.6 0.8 sum_sections.1
  28.5 15.4 %all-to-all-start.1 = ((bf16[32,4,8,128]{3,2,1,0:T(8,128)(2,1)}), bf16[32,4,8,128]{3,2,1,0:T(8,128)(2,1)S(1)}, u32[]{:S(2)}, u32[]{:S(2)}) async-start(bf16[32,4,8,128]{3,2,1,0:T(8,128)(2,1)} %sum_sections.1), calls=%async_computation.1 | async-start | bytes 524288 | tf_op jit(solution)/shard_map/all_to_all | solution.py:380
  43.9 0.0 copy-done
  43.9 0.0 copy-start.5
  43.9 0.0 copy-start.6
  43.9 0.0 copy-start.7
  43.9 0.0 copy-start.9
  43.9 1.3 %regroup.1.grouped = bf16[4,512,512]{2,1,0:T(8,128)(2,1)S(1)} custom-call(bf16[4,512,512]{2,1,0:T(8,128)(2,1)S(1)} %copy-done), custom_call_target="tpu_custom_call" | custom-call | tf_op jit(solution)/shard_map/regroup/pallas_call | solution.py:252
  45.2 0.0 copy-start.1
  45.3 1.3 %copy-done.1 = bf16[4,512,512]{2,1,0:T(8,128)(2,1)} copy-done((bf16[4,512,512]{2,1,0:T(8,128)(2,1)}, bf16[4,512,512]{2,1,0:T(8,128)(2,1)S(1)}, u32[]{:S(2)}) %copy-start.1) | copy-done | bytes 2097176
  46.6 0.0 copy-done.5
  46.6 0.0 copy-done.6
  46.6 0.0 copy-done.7
  46.6 0.0 copy-done.9
  46.6 2.6 %make_basis.1 = (bf16[1024,1024]{1,0:T(8,128)(2,1)S(1)}, bf16[128,1024]{1,0:T(8,128)(2,1)S(1)}, f32[8,1024]{1,0:T(8,128)S(1)}) custom-call(s32[1]{0:T(128)} %bitcast.4.here, s32[1]{0:T(128)} %bitcast.5.at_x, s32[4]{0:T(128)S(1)} %copy-done.9, s32[4,1024]{1,0:T(4,128)S(1)} %copy-done.5, f32[4,1024]{1,0:T(4,128)S(1)} %copy-done.6, f32[4,1024]{1,0:T(4,128)S(1)} %copy-done.7, ...), custom_call_target="tpu_custom_call" | custom-call | tf_op jit(solution)/shard_map/make_basis/pallas_call | solution.py:178
  49.2 17.4 %all-to-all-done.1 = bf16[32,4,8,128]{3,2,1,0:T(8,128)(2,1)S(1)} async-done(((bf16[32,4,8,128]{3,2,1,0:T(8,128)(2,1)}), bf16[32,4,8,128]{3,2,1,0:T(8,128)(2,1)S(1)}, u32[]{:S(2)}, u32[]{:S(2)}) %all-to-all-start.1) | async-done | bytes 262176 | tf_op jit(solution)/shard_map/all_to_all | solution.py:380
  66.6 1.3 %observe.1 = (bf16[1024,128]{1,0:T(8,128)(2,1)S(1)}, bf16[24,128]{1,0:T(8,128)(2,1)S(1)}) custom-call(bf16[1024,1024]{1,0:T(8,128)(2,1)S(1)} %get-tuple-element.17.by_wave, bf16[1024,128]{1,0:T(8,128)(2,1)S(1)} %bitcast.15, bf16[128,1024]{1,0:T(8,128)(2,1)S(1)} %get-tuple-element.19.kern, f32[8,1024]{1,0:T(8,128)S(1)} %get-tuple-element.20.lines), custom_call_target="tpu_custom_call" | custom-call | tf_op jit(solution)/shard_map/observe/pallas_call | solution.py:212
  67.9 0.0 copy-start.2
  67.9 0.0 copy-start.3
  67.9 0.0 copy-start.4
  67.9 0.0 copy-start.8
  67.9 26.0 %all_to_all.21 = bf16[32,4,8,128]{3,2,1,0:T(8,128)(2,1)S(1)} all-to-all(bf16[32,4,8,128]{3,2,1,0:T(8,128)(2,1)S(1)} %bitcast.16), channel_id=1, replica_groups=mesh['section'=4,'z'=16,'x'=4,'core'=2] {'z','core'}, dimensions={0} | all-to-all | bytes 524288 | tf_op jit(solution)/shard_map/all_to_all | solution.py:392
  93.9 0.4 pack.1
  94.3 20.4 %all_to_all.22.packets = bf16[16,280,128]{2,1,0:T(8,128)(2,1)S(1)} all-to-all(bf16[16,280,128]{2,1,0:T(8,128)(2,1)S(1)} %pack.1), channel_id=1, replica_groups=mesh['section'=4,'z'=16,'x'=4,'core'=2] {'section','x'}, dimensions={0} | all-to-all | bytes 2293760 | tf_op jit(solution)/shard_map/all_to_all | solution.py:396
  114.7 0.0 copy-done.2
  114.7 0.0 copy-done.3
  114.7 0.0 copy-done.4
  114.8 0.0 copy-done.8
  114.8 2.3 %backward_gradient.1 = (bf16[4,256,512]{2,1,0:T(8,128)(2,1)}, f32[4,1024]{1,0:T(4,128)}) custom-call(bf16[16,280,128]{2,1,0:T(8,128)(2,1)S(1)} %all_to_all.22.packets, bf16[4,512,512]{2,1,0:T(8,128)(2,1)S(1)} %copy-done.2, bf16[4,256,512]{2,1,0:T(8,128)(2,1)S(1)} %bitcast.13, f32[1,512]{1,0:T(1,128)S(1)} %copy-done.8, bf16[128,128]{1,0:T(8,128)(2,1)S(1)} %bitcast.18), custom_call_target="tpu_custom_call" | custom-call | tf_op jit(solution)/shard_map/backward_gradient/pallas_call | solution.py:339
Async XLA Ops:
  4.3 39.5 %copy-start = (bf16[4,512,512]{2,1,0:T(8,128)(2,1)S(1)}, bf16[4,512,512]{2,1,0:T(8,128)(2,1)}, u32[]{:S(2)}) copy-start(bf16[4,512,512]{2,1,0:T(8,128)(2,1)} %legendre.3) | copy-start | bytes 6291460
  28.5 38.1 %all-to-all-start.1 = ((bf16[32,4,8,128]{3,2,1,0:T(8,128)(2,1)}), bf16[32,4,8,128]{3,2,1,0:T(8,128)(2,1)S(1)}, u32[]{:S(2)}, u32[]{:S(2)}) async-start(bf16[32,4,8,128]{3,2,1,0:T(8,128)(2,1)} %sum_sections.1), calls=%async_computation.1 | async-start | bytes 524288 | tf_op jit(solution)/shard_map/all_to_all | solution.py:380
  43.9 2.7 %copy-start.5 = (s32[4,1024]{1,0:T(4,128)S(1)}, s32[4,1024]{1,0:T(4,128)}, u32[]{:S(2)}) copy-start(s32[4,1024]{1,0:T(4,128)} %obs_lon.1) | copy-start | bytes 49156
  43.9 2.7 %copy-start.6 = (f32[4,1024]{1,0:T(4,128)S(1)}, f32[4,1024]{1,0:T(4,128)}, u32[]{:S(2)}) copy-start(f32[4,1024]{1,0:T(4,128)} %value.1) | copy-start | bytes 49156
  43.9 2.7 %copy-start.7 = (f32[4,1024]{1,0:T(4,128)S(1)}, f32[4,1024]{1,0:T(4,128)}, u32[]{:S(2)}) copy-start(f32[4,1024]{1,0:T(4,128)} %weight.1) | copy-start | bytes 49156
  43.9 2.7 %copy-start.9 = (s32[4]{0:T(128)S(1)}, s32[4]{0:T(128)}, u32[]{:S(2)}) copy-start(s32[4]{0:T(128)} %count.1) | copy-start | bytes 52
  45.2 1.3 %copy-start.1 = (bf16[4,512,512]{2,1,0:T(8,128)(2,1)}, bf16[4,512,512]{2,1,0:T(8,128)(2,1)S(1)}, u32[]{:S(2)}) copy-start(bf16[4,512,512]{2,1,0:T(8,128)(2,1)S(1)} %regroup.1.grouped) | copy-start | bytes 6291460
  67.9 46.9 %copy-start.2 = (bf16[4,512,512]{2,1,0:T(8,128)(2,1)S(1)}, bf16[4,512,512]{2,1,0:T(8,128)(2,1)}, u32[]{:S(2)}) copy-start(bf16[4,512,512]{2,1,0:T(8,128)(2,1)} %copy-done.1) | copy-start | bytes 6291460
  67.9 46.9 %copy-start.3 = (bf16[1,4,2,128,512]{4,3,2,1,0:T(8,128)(2,1)S(1)}, bf16[1,4,2,128,512]{4,3,2,1,0:T(8,128)(2,1)}, u32[]{:S(2)}) copy-start(bf16[1,4,2,128,512]{4,3,2,1,0:T(8,128)(2,1)} %param.9) | copy-start | bytes 3145732
  67.9 46.9 %copy-start.4 = (bf16[1,128,128]{2,1,0:T(8,128)(2,1)S(1)}, bf16[1,128,128]{2,1,0:T(8,128)(2,1)}, u32[]{:S(2)}) copy-start(bf16[1,128,128]{2,1,0:T(8,128)(2,1)} %param.12) | copy-start | bytes 98308
  67.9 46.9 %copy-start.8 = (f32[1,512]{1,0:T(1,128)S(1)}, f32[1,512]{1,0:T(1,128)}, u32[]{:S(2)}) copy-start(f32[1,512]{1,0:T(1,128)} %spread.3) | copy-start | bytes 6148
